TPU v7x, 32 devices: a whole 2x2x4 slice. The times are simulated.
32 devices in a mesh: date: 8 (over z, x), az: 4 (over y, core).
Axes of the slice: x: 2, y: 2, z: 4, core: 2. Of those that a mesh axis runs over, the one named last changes fastest.
Arguments:
- slc: float32 [48, 2, 32, 1024], P('date', None, 'az'), may hold values from -12 to 12
- pairs: int32 [2, 512, 2], replicated, may hold values from 0 to 47, as said below
Outputs:
- interferogram: float32 [2, 512, 2, 8, 64], P(None, 'date', None, 'az')
- coherence: float32 [2, 512, 8, 64], P(None, 'date', 'az')
Inputs may be any that keep to these rules, and one draw needn't show every extreme that they name: In each round the two dates of a pair differ; the pairs in the block of 64 rows of one device name exactly 8 distinct dates, and at most 2 distinct dates out of any one block of 6 dates, exactly 2 out of some block.
All inputs are finite; a program needn't handle non-finite values.
Results may differ from a plain program's by a relative error of at most 0.0014.
Values may be sent and summed in bfloat16 or wider, within the bound.
A program may use at most 64 MiB of HBM per device.

v0:
```python
import jax
import jax.numpy as jnp
from jax import lax
from jax.sharding import PartitionSpec as P

CAP = 2


def with_halo(shard, sides, width):
    for axis, dim in sides:
        peers, length = (lax.axis_size(axis), shard.shape[dim])
        up = [(i, (i + 1) % peers) for i in range(peers - 1)]
        down = [(j, i) for i, j in up]
        last = lax.slice_in_dim(shard, length - width, length, axis=dim)
        first = lax.slice_in_dim(shard, 0, width, axis=dim)
        before = lax.ppermute(last, axis, up)
        after = lax.ppermute(first, axis, down)
        shard = jnp.concatenate([before, shard, after], axis=dim)
    return shard


def multilook(field):
    shape = field.shape
    blocks = field.reshape(shape[:-2] + (shape[-2] // 4, 4, shape[-1] // 16, 16))
    return blocks.mean(axis=(-3, -1))


def pair_looks(tiles):
    first = tiles[:, 0].astype(jnp.float32)
    second = tiles[:, 1].astype(jnp.float32)
    first_re, first_im = (first[:, 0], first[:, 1])
    second_re, second_im = (second[:, 0], second[:, 1])
    prod_re = first_re * second_re + first_im * second_im
    prod_im = first_im * second_re - first_re * second_im
    power_a = first_re * first_re + first_im * first_im
    power_b = second_re * second_re + second_im * second_im
    return jnp.stack(
        [multilook(prod_re), multilook(prod_im), multilook(power_a), multilook(power_b)], axis=1
    )


def coherence_from(padded):
    lines = padded.shape[-2] - 4
    columns = padded.shape[-1]
    az_sum = padded[..., 0:lines, :]
    for offset in range(1, 5):
        az_sum = az_sum + padded[..., offset : offset + lines, :]
    widths = [(0, 0)] * (az_sum.ndim - 1) + [(2, 2)]
    wide = jnp.pad(az_sum, widths)
    boxed = wide[..., 0:columns]
    for offset in range(1, 5):
        boxed = boxed + wide[..., offset : offset + columns]
    numer = jnp.sqrt(boxed[..., 0, :, :] ** 2 + boxed[..., 1, :, :] ** 2)
    return numer / jnp.sqrt(boxed[..., 2, :, :] * boxed[..., 3, :, :])


def per_device(slc, pairs):
    date_count = lax.axis_size("date")
    own_index = lax.axis_index("date")
    date_dev = slc.shape[0]
    pair_dev = pairs.shape[1] // date_count
    tile_shape = slc.shape[1:]
    quantized = lax.optimization_barrier(slc.astype(jnp.bfloat16))
    all_ids = jnp.arange(date_count * date_dev, dtype=jnp.int32)
    local_ids = own_index * date_dev + jnp.arange(date_dev, dtype=jnp.int32)
    local_pos = jnp.arange(date_dev, dtype=jnp.int32)
    slot_ids = jnp.arange(CAP, dtype=jnp.int32)
    looks_list = []
    for round_index in range(pairs.shape[0]):
        block = pairs[round_index]
        own_pairs = lax.dynamic_slice_in_dim(block, own_index * pair_dev, pair_dev, 0)
        entries = own_pairs.reshape(-1)
        wanted = block.reshape(date_count, 2 * pair_dev)
        needed = jnp.any(wanted[:, :, None] == local_ids[None, None, :], axis=1).astype(jnp.int32)
        ranks = jnp.cumsum(needed, axis=1) - needed
        picked = needed[:, None, :] * (ranks[:, None, :] == slot_ids[None, :, None]).astype(
            jnp.int32
        )
        source_local = jnp.sum(picked * local_pos[None, None, :], axis=2)
        present = jnp.sum(picked, axis=2) > 0
        outgoing = jnp.take(quantized, source_local.reshape(-1), axis=0).reshape(
            (date_count, CAP) + tile_shape
        )
        outgoing = jnp.where(present[:, :, None, None, None], outgoing, jnp.zeros((), jnp.bfloat16))
        incoming = lax.all_to_all(outgoing, "date", split_axis=0, concat_axis=0, tiled=True)
        matches = entries[:, None] == all_ids[None, :]
        my_need = jnp.any(matches, axis=0).astype(jnp.int32).reshape(date_count, date_dev)
        my_rank = (jnp.cumsum(my_need, axis=1) - my_need).reshape(-1)
        entry_slot = jnp.sum(jnp.where(matches, my_rank[None, :], 0), axis=1)
        position = entries // date_dev * CAP + entry_slot
        fetched = jnp.take(incoming.reshape((date_count * CAP,) + tile_shape), position, axis=0)
        looks = pair_looks(fetched.reshape((pair_dev, 2) + tile_shape))
        looks_list.append(looks)
    stacked = jnp.stack(looks_list, axis=0)
    padded = with_halo(stacked, (("az", 3),), 2)
    coherence = coherence_from(padded)
    interferogram = stacked[:, :, 0:2]
    return (interferogram, coherence)


def solution(mesh):
    return jax.shard_map(
        per_device,
        mesh=mesh,
        in_specs=(P("date", None, "az", None), P()),
        out_specs=(P(None, "date", None, "az", None), P(None, "date", "az", None)),
        check_vma=False,
    )
```

profile of v0, /device:TPU:1, one launch (start us, length us, event | category | flops | bytes accessed | tf_op | source)
XLA Modules:
  0.0 115.7 jit_solution(5174110014193143739)
XLA Ops:
  2.7 1.0 convert_element_type.86
  5.4 6.3 %all-to-all-start.1 = ((bf16[8,2,2,8,1024]{4,3,2,1,0:T(8,128)(2,1)}), bf16[8,2,2,8,1024]{4,3,2,1,0:T(8,128)(2,1)S(1)}, u32[]{:S(2)}, u32[]{:S(2)}) async-start(bf16[8,2,2,8,1024]{4,3,2,1,0:T(8,128)(2,1)} %broadcast_select_fusion.4), calls=%async_computation.1 | async-start | bytes 1048576 | tf_op jit(solution)/shard_map/all_to_all | solution.py:85
  15.5 9.7 %all-to-all-done.1 = bf16[8,2,2,8,1024]{4,3,2,1,0:T(8,128)(2,1)S(1)} async-done(((bf16[8,2,2,8,1024]{4,3,2,1,0:T(8,128)(2,1)}), bf16[8,2,2,8,1024]{4,3,2,1,0:T(8,128)(2,1)S(1)}, u32[]{:S(2)}, u32[]{:S(2)}) %all-to-all-start.1) | async-done | bytes 524320 | tf_op jit(solution)/shard_map/all_to_all | solution.py:85
  25.2 4.9 %all-to-all-start = ((bf16[8,2,2,8,1024]{4,3,2,1,0:T(8,128)(2,1)}), bf16[8,2,2,8,1024]{4,3,2,1,0:T(8,128)(2,1)S(1)}, u32[]{:S(2)}, u32[]{:S(2)}) async-start(bf16[8,2,2,8,1024]{4,3,2,1,0:T(8,128)(2,1)} %broadcast_select_fusion.5), calls=%async_computation | async-start | bytes 1048576 | tf_op jit(solution)/shard_map/all_to_all | solution.py:85
  30.0 2.7 %gather_fusion.3 = bf16[128,2,8,1024]{3,2,1,0:T(8,128)(2,1)} fusion(bf16[16,2,8,1024]{3,2,1,0:T(8,128)(2,1)S(1)} %bitcast.60, s32[1024]{0:T(1024)S(1)} %pad_clamp_fusion), kind=kCustom, calls=%fused_computation.3.clone | custom fusion | bytes 8389120 | tf_op jit(solution)/shard_map/jit(_take)/gather | solution.py:91
  32.8 2.6 %broadcast_select_fusion = bf16[128,2,8,1024]{3,2,1,0:T(8,128)(2,1)S(1)} fusion(bf16[128,2,8,1024]{3,2,1,0:T(8,128)(2,1)} %gather_fusion.3, pred[128]{0:T(512)(128)(4,1)S(1)} %get-tuple-element.20), kind=kLoop, calls=%fused_computation.4 | loop fusion | flops 2097152 | bytes 8388736 | tf_op jit(solution)/shard_map/jit(_take)/select_n | solution.py:91
  35.4 1.1 fusion.1
  36.5 3.7 %multiply_add_fusion.2 = (f32[64,1,8,1024]{3,2,1,0:T(8,128)S(1)}, f32[64,1,8,1024]{3,2,1,0:T(8,128)}, f32[64,1,8,1024]{3,2,1,0:T(8,128)}, f32[64,1,8,1024]{3,2,1,0:T(8,128)}) fusion(f32[64,2,8,1024]{3,2,1,0:T(8,128)S(1)} %get-tuple-element.31, f32[64,2,8,1024]{3,2,1,0:T(8,128)S(1)} %get-tuple-element.30), kind=kLoop, calls=%fused_computation.17 | loop fusion | flops 6291456 | bytes 16777216 | tf_op jit(solution)/shard_map/add | solution.py:33
  40.2 3.8 %copy.65 = f32[64,1,8,1024]{0,3,2,1:T(8,128)} copy(f32[64,1,8,1024]{3,2,1,0:T(8,128)} %get-tuple-element.29) | data formatting | bytes 4194304 | tf_op jit(solution)/shard_map/add | solution.py:36
  44.0 3.8 %copy.64 = f32[64,1,8,1024]{0,3,2,1:T(8,128)} copy(f32[64,1,8,1024]{3,2,1,0:T(8,128)} %get-tuple-element.28) | data formatting | bytes 4194304 | tf_op jit(solution)/shard_map/add | solution.py:35
  47.8 2.6 %reduce_sum.139 = f32[64,2,64]{0,2,1:T(8,128)S(1)} reduce(f32[64,2,4,64,16]{0,4,3,2,1:T(8,128)} %bitcast.64, f32[]{:T(128)} %constant.73.clone.1), dimensions={2,4}, to_apply=%region_21.24 | reduce | flops 516096 | bytes 2129924 | tf_op jit(solution)/shard_map/reduce_sum | solution.py:25
  50.5 2.6 %reduce_sum.138 = f32[64,2,64]{0,2,1:T(8,128)S(1)} reduce(f32[64,2,4,64,16]{0,4,3,2,1:T(8,128)} %bitcast.65, f32[]{:T(128)} %constant.73.clone.1), dimensions={2,4}, to_apply=%region_20.23 | reduce | flops 516096 | bytes 2129924 | tf_op jit(solution)/shard_map/reduce_sum | solution.py:25
  53.1 3.8 %copy.63 = f32[64,1,8,1024]{0,3,2,1:T(8,128)} copy(f32[64,1,8,1024]{3,2,1,0:T(8,128)} %get-tuple-element.25) | data formatting | bytes 4194304 | tf_op jit(solution)/shard_map/sub | solution.py:34
  56.9 2.6 %reduce_sum.137 = f32[64,2,64]{0,2,1:T(8,128)S(1)} reduce(f32[64,2,4,64,16]{0,4,3,2,1:T(8,128)} %bitcast.67, f32[]{:T(128)} %constant.73.clone.1), dimensions={2,4}, to_apply=%region_19.22 | reduce | flops 516096 | bytes 2129924 | tf_op jit(solution)/shard_map/reduce_sum | solution.py:25
  59.5 2.8 %copy.62 = f32[64,1,8,1024]{0,3,2,1:T(8,128)} copy(f32[64,1,8,1024]{3,2,1,0:T(8,128)S(1)} %get-tuple-element.24) | data formatting | bytes 4194304 | tf_op jit(solution)/shard_map/add | solution.py:33
  62.3 2.6 %reduce_sum.136 = f32[64,2,64]{0,2,1:T(8,128)S(1)} reduce(f32[64,2,4,64,16]{0,4,3,2,1:T(8,128)} %bitcast.68, f32[]{:T(128)} %constant.73.clone.1), dimensions={2,4}, to_apply=%region_18.21 | reduce | flops 516096 | bytes 2129924 | tf_op jit(solution)/shard_map/reduce_sum | solution.py:25
  65.0 2.7 %gather_fusion.1 = bf16[128,2,8,1024]{3,2,1,0:T(8,128)(2,1)} fusion(bf16[16,2,8,1024]{3,2,1,0:T(8,128)(2,1)S(1)} %bitcast.61, s32[1024]{0:T(1024)S(1)} %pad_clamp_fusion.2), kind=kCustom, calls=%fused_computation.1.clone | custom fusion | bytes 8389120 | tf_op jit(solution)/shard_map/jit(_take)/gather | solution.py:91
  67.7 2.6 %broadcast_select_fusion.1 = bf16[128,2,8,1024]{3,2,1,0:T(8,128)(2,1)S(1)} fusion(bf16[128,2,8,1024]{3,2,1,0:T(8,128)(2,1)} %gather_fusion.1, pred[128]{0:T(512)(128)(4,1)S(1)} %get-tuple-element.22), kind=kLoop, calls=%fused_computation.5 | loop fusion | flops 2097152 | bytes 8388736 | tf_op jit(solution)/shard_map/jit(_take)/select_n | solution.py:91
  70.3 1.1 fusion.3
  71.4 3.7 %multiply_add_fusion.5 = (f32[64,1,8,1024]{3,2,1,0:T(8,128)S(1)}, f32[64,1,8,1024]{3,2,1,0:T(8,128)}, f32[64,1,8,1024]{3,2,1,0:T(8,128)}, f32[64,1,8,1024]{3,2,1,0:T(8,128)}) fusion(f32[64,2,8,1024]{3,2,1,0:T(8,128)S(1)} %get-tuple-element.35, f32[64,2,8,1024]{3,2,1,0:T(8,128)S(1)} %get-tuple-element.34), kind=kLoop, calls=%fused_computation.21 | loop fusion | flops 6291456 | bytes 16777216 | tf_op jit(solution)/shard_map/add | solution.py:33
  75.1 3.8 %copy.56 = f32[64,1,8,1024]{0,3,2,1:T(8,128)} copy(f32[64,1,8,1024]{3,2,1,0:T(8,128)} %get-tuple-element.33) | data formatting | bytes 4194304 | tf_op jit(solution)/shard_map/add | solution.py:36
  78.9 2.6 %reduce_sum.132 = f32[64,2,64]{0,2,1:T(8,128)S(1)} reduce(f32[64,2,4,64,16]{0,4,3,2,1:T(8,128)} %bitcast.69, f32[]{:T(128)} %constant.73.clone.1), dimensions={2,4}, to_apply=%region_10.13 | reduce | flops 516096 | bytes 2129924 | tf_op jit(solution)/shard_map/reduce_sum | solution.py:25
  81.5 4.0 %copy.55 = f32[64,1,8,1024]{0,3,2,1:T(8,128)} copy(f32[64,1,8,1024]{3,2,1,0:T(8,128)} %get-tuple-element.32) | data formatting | bytes 4194304 | tf_op jit(solution)/shard_map/add | solution.py:35
  85.6 2.6 %reduce_sum.131 = f32[64,2,64]{0,2,1:T(8,128)S(1)} reduce(f32[64,2,4,64,16]{0,4,3,2,1:T(8,128)} %bitcast.70, f32[]{:T(128)} %constant.73.clone.1), dimensions={2,4}, to_apply=%region_9.12 | reduce | flops 516096 | bytes 2129924 | tf_op jit(solution)/shard_map/reduce_sum | solution.py:25
  88.2 3.8 %copy.54 = f32[64,1,8,1024]{0,3,2,1:T(8,128)} copy(f32[64,1,8,1024]{3,2,1,0:T(8,128)} %get-tuple-element.27) | data formatting | bytes 4194304 | tf_op jit(solution)/shard_map/sub | solution.py:34
  92.0 2.6 %reduce_sum.130 = f32[64,2,64]{0,2,1:T(8,128)S(1)} reduce(f32[64,2,4,64,16]{0,4,3,2,1:T(8,128)} %bitcast.71, f32[]{:T(128)} %constant.73.clone.1), dimensions={2,4}, to_apply=%region_8.11 | reduce | flops 516096 | bytes 2129924 | tf_op jit(solution)/shard_map/reduce_sum | solution.py:25
  94.6 2.8 %copy.53 = f32[64,1,8,1024]{0,3,2,1:T(8,128)} copy(f32[64,1,8,1024]{3,2,1,0:T(8,128)S(1)} %get-tuple-element.26) | data formatting | bytes 4194304 | tf_op jit(solution)/shard_map/add | solution.py:33
  97.4 2.6 %reduce_sum.129 = f32[64,2,64]{0,2,1:T(8,128)S(1)} reduce(f32[64,2,4,64,16]{0,4,3,2,1:T(8,128)} %bitcast.66, f32[]{:T(128)} %constant.73.clone.1), dimensions={2,4}, to_apply=%region_7.10 | reduce | flops 516096 | bytes 2129924 | tf_op jit(solution)/shard_map/reduce_sum | solution.py:25
  100.1 3.8 %collective-permute-start = (f32[2,64,4,2,64]{1,4,3,2,0:T(8,128)S(1)}, f32[2,64,4,2,64]{1,4,3,2,0:T(8,128)S(1)}, u32[]{:S(2)}, u32[]{:S(2)}) collective-permute-start(f32[2,64,4,2,64]{1,4,3,2,0:T(8,128)S(1)} %pad_maximum_fusion), channel_id=1, source_target_pairs={{0,1},{1,2},{2,3},{4,5},{5,6},{6,7},{8,9},{9,10},{10,11},{12,13},{... | collective-permute-start | bytes 786440 | tf_op jit(solution)/shard_map/ppermute | solution.py:16
  104.0 1.9 %collective-permute-start.1 = (f32[2,64,4,2,64]{1,4,3,2,0:T(8,128)S(1)}, f32[2,64,4,2,64]{1,4,3,2,0:T(8,128)S(1)}, u32[]{:S(2)}, u32[]{:S(2)}) collective-permute-start(f32[2,64,4,2,64]{1,4,3,2,0:T(8,128)S(1)} %pad_maximum_fusion), channel_id=1, source_target_pairs={{1,0},{2,1},{3,2},{5,4},{6,5},{7,6},{9,8},{10,9},{11,10},{13,12},{... | collective-permute-start | bytes 786440 | tf_op jit(solution)/shard_map/ppermute | solution.py:17
  106.8 3.3 %collective-permute-done = f32[2,64,4,2,64]{1,4,3,2,0:T(8,128)S(1)} collective-permute-done((f32[2,64,4,2,64]{1,4,3,2,0:T(8,128)S(1)}, f32[2,64,4,2,64]{1,4,3,2,0:T(8,128)S(1)}, u32[]{:S(2)}, u32[]{:S(2)}) %collective-permute-start) | collective-permute-done | bytes 262176 | tf_op jit(solution)/shard_map/ppermute | solution.py:16
  110.1 4.4 %collective-permute-done.1 = f32[2,64,4,2,64]{1,4,3,2,0:T(8,128)S(1)} collective-permute-done((f32[2,64,4,2,64]{1,4,3,2,0:T(8,128)S(1)}, f32[2,64,4,2,64]{1,4,3,2,0:T(8,128)S(1)}, u32[]{:S(2)}, u32[]{:S(2)}) %collective-permute-start.1) | collective-permute-done | bytes 262176 | tf_op jit(solution)/shard_map/ppermute | solution.py:17
  (75 shorter events, 9.4 us)
Async XLA Ops:
  5.4 19.8 %all-to-all-start.1 = ((bf16[8,2,2,8,1024]{4,3,2,1,0:T(8,128)(2,1)}), bf16[8,2,2,8,1024]{4,3,2,1,0:T(8,128)(2,1)S(1)}, u32[]{:S(2)}, u32[]{:S(2)}) async-start(bf16[8,2,2,8,1024]{4,3,2,1,0:T(8,128)(2,1)} %broadcast_select_fusion.4), calls=%async_computation.1 | async-start | bytes 1048576 | tf_op jit(solution)/shard_map/all_to_all | solution.py:85
  25.2 39.8 %all-to-all-start = ((bf16[8,2,2,8,1024]{4,3,2,1,0:T(8,128)(2,1)}), bf16[8,2,2,8,1024]{4,3,2,1,0:T(8,128)(2,1)S(1)}, u32[]{:S(2)}, u32[]{:S(2)}) async-start(bf16[8,2,2,8,1024]{4,3,2,1,0:T(8,128)(2,1)} %broadcast_select_fusion.5), calls=%async_computation | async-start | bytes 1048576 | tf_op jit(solution)/shard_map/all_to_all | solution.py:85
  100.1 9.9 %collective-permute-start = (f32[2,64,4,2,64]{1,4,3,2,0:T(8,128)S(1)}, f32[2,64,4,2,64]{1,4,3,2,0:T(8,128)S(1)}, u32[]{:S(2)}, u32[]{:S(2)}) collective-permute-start(f32[2,64,4,2,64]{1,4,3,2,0:T(8,128)S(1)} %pad_maximum_fusion), channel_id=1, source_target_pairs={{0,1},{1,2},{2,3},{4,5},{5,6},{6,7},{8,9},{9,10},{10,11},{12,13},{... | collective-permute-start | bytes 786440 | tf_op jit(solution)/shard_map/ppermute | solution.py:16
  104.0 10.5 %collective-permute-start.1 = (f32[2,64,4,2,64]{1,4,3,2,0:T(8,128)S(1)}, f32[2,64,4,2,64]{1,4,3,2,0:T(8,128)S(1)}, u32[]{:S(2)}, u32[]{:S(2)}) collective-permute-start(f32[2,64,4,2,64]{1,4,3,2,0:T(8,128)S(1)} %pad_maximum_fusion), channel_id=1, source_target_pairs={{1,0},{2,1},{3,2},{5,4},{6,5},{7,6},{9,8},{10,9},{11,10},{13,12},{... | collective-permute-start | bytes 786440 | tf_op jit(solution)/shard_map/ppermute | solution.py:17
where the time goes:
time: 117 us; the launch traced here: 116 us
  other arithmetic  40.6 us (35%)
  local copies, waits for them, and re-layouts  39.7 us (34%)
  waiting for transfers between devices  17.4 us (15%)
  starting transfers between devices  16.9 us (14%)
    reduce_sum x8, other arithmetic, multilook(): return blocks.mean(axis=(-3, -1))  20.8 us
    all_to_all x2, starting transfers between devices, per_device(): lax.all_to_all(outgoing, 'date', split_axis=0, concat_axis=0, tiled=True)  11.2 us
    all_to_all x2, waiting for transfers between devices, per_device(): lax.all_to_all(outgoing, 'date', split_axis=0, concat_axis=0, tiled=True)  9.71 us
    add x2, local copies, waits for them, and re-layouts, pair_looks(): power_a = first_re * first_re + first_im * first_im  7.86 us
    sub x2, local copies, waits for them, and re-layouts, pair_looks(): prod_im = first_im * second_re - first_re * second_im  7.68 us
    add x2, local copies, waits for them, and re-layouts, pair_looks(): power_b = second_re * second_re + second_im * second_im  7.67 us
    add x2, other arithmetic, pair_looks(): prod_re = first_re * second_re + first_im * second_im  7.32 us
    add x2, local copies, waits for them, and re-layouts, pair_looks(): prod_re = first_re * second_re + first_im * second_im  5.52 us
  transfers between devices with their start and end apart: 4, of which 3 were waited for; matrix products, arithmetic and copies ran while one was open for 34% of the time, Pallas kernels for 0%

commit v1 on v0

--- a/solution.py
+++ b/solution.py
@@ -1,6 +1,8 @@
 import jax
 import jax.numpy as jnp
 from jax import lax
+from jax.experimental import pallas as pl
+from jax.experimental.pallas import tpu as pltpu
 from jax.sharding import PartitionSpec as P
 
 CAP = 2
@@ -54,7 +56,7 @@
     return numer / jnp.sqrt(boxed[..., 2, :, :] * boxed[..., 3, :, :])
 
 
-def per_device(slc, pairs):
+def per_device_general(slc, pairs):
     date_count = lax.axis_size("date")
     own_index = lax.axis_index("date")
     date_dev = slc.shape[0]
@@ -98,6 +100,223 @@
     return (interferogram, coherence)
 
 
+LINES, SAMPLES = 4, 16
+STEPS = ((0, 2), (0, 1), (1, 8), (1, 4), (1, 2), (1, 1))
+
+
+def iota(shape, dim):
+    return lax.broadcasted_iota(jnp.int32, shape, dim)
+
+
+def place_of(leaf):
+    bit = [(leaf >> n) & 1 for n in range(6)]
+    return 32 * bit[3] + 16 * bit[4] + 8 * bit[5] + 4 * bit[2] + 2 * bit[0] + bit[1]
+
+
+def rolled(x, shift, dim):
+    return pltpu.roll(x, shift % x.shape[dim], dim)
+
+
+def join(one, two, dim, dist):
+    low = (iota(one.shape, dim) & dist) == 0
+    kept = jnp.where(low, one, two)
+    other = jnp.where(low, two, one)
+    return kept + jnp.where(low, rolled(other, -dist, dim), rolled(other, dist, dim))
+
+
+def cell_sums(real, imag):
+    count = len(real)
+    couples = [(i, j) for i in range(count) for j in range(i + 1, count)]
+
+    def quantity(place):
+        if place < len(couples):
+            i, j = couples[place]
+            return real[i] * real[j] + imag[i] * imag[j]
+        place -= len(couples)
+        if place < len(couples):
+            i, j = couples[place]
+            return imag[i] * real[j] - real[i] * imag[j]
+        i = place - len(couples)
+        return real[i] * real[i] + imag[i] * imag[i]
+
+    def build(level, base):
+        if level == 0:
+            return quantity(place_of(base))
+        one = build(level - 1, base)
+        two = build(level - 1, base + (1 << (level - 1)))
+        return join(one, two, *STEPS[level - 1])
+
+    return build(len(STEPS), 0)
+
+
+def exact_dot(a, b):
+    return lax.dot_general(
+        a,
+        b,
+        (((1,), (0,)), ((), ())),
+        precision=lax.Precision.HIGHEST,
+        preferred_element_type=jnp.float32,
+    )
+
+
+def cells_last(x):
+    shape = (128, 128)
+    src, dst = iota(shape, 0), iota(shape, 1)
+    hit = dst == (src % SAMPLES) * (128 // SAMPLES) + src // SAMPLES
+    return exact_dot(x, jnp.where(hit, 1.0 / (LINES * SAMPLES), 0.0).astype(jnp.float32))
+
+
+def table_of(tiles):
+    lane, sub = iota((8, 128), 1), iota((8, 128), 0)
+    tiles = list(tiles)
+    for b in range(3):
+        dist = 8 << b
+        low = (lane & dist) == 0
+        for j in range(8):
+            if not j >> b & 1:
+                one, two = tiles[j], tiles[j | 1 << b]
+                tiles[j] = jnp.where(low, one, rolled(two, dist, 1))
+                tiles[j | 1 << b] = jnp.where(low, rolled(one, -dist, 1), two)
+    same = (sub < 4) == (lane < 64)
+    return [jnp.where(same, t, rolled(rolled(t, 4, 0), 64, 1)) for t in tiles]
+
+
+def box_of(own, before, after):
+    lane = iota(own.shape, 1)
+    first = lane < 64
+    both = own + rolled(own, 64, 1)
+    both = both + jnp.where(first, before + rolled(before, 64, 1), before)
+    both = both + jnp.where(first, after, after + rolled(after, 64, 1))
+    cell = lane & 63
+    out = both
+    for o in (-2, -1, 1, 2):
+        valid = (cell + o >= 0) & (cell + o < 64)
+        out = out + jnp.where(valid, rolled(both, -o, 1), 0.0)
+    return out
+
+
+def expand(looks, boxed, rank_a, rank_b, count):
+    rows = rank_a.shape[0]
+    total = looks.shape[0]
+    q = iota((rows, total), 1)
+    low, high = jnp.minimum(rank_a, rank_b), jnp.maximum(rank_a, rank_b)
+    place = ((low * (2 * count - 1 - low)) >> 1) + high - low - 1
+    couples = count * (count - 1) // 2
+    sel_re = jnp.where(q == place, 1.0, 0.0)
+    sel_im = jnp.where(q == place + couples, jnp.where(rank_a < rank_b, 1.0, -1.0), 0.0)
+    sel_a = jnp.where(q == rank_a + 2 * couples, 1.0, 0.0)
+    sel_b = jnp.where(q == rank_b + 2 * couples, 1.0, 0.0)
+    means = exact_dot(jnp.concatenate([sel_re, sel_im], 0), looks)
+    sums = exact_dot(jnp.concatenate([sel_re, sel_im, sel_a, sel_b], 0), boxed)
+    box_re, box_im, box_a, box_b = (sums[n * rows : (n + 1) * rows] for n in range(4))
+    coherence = jnp.sqrt(box_re * box_re + box_im * box_im) / jnp.sqrt(box_a * box_b)
+    return means[:rows], means[rows:], coherence
+
+
+def sums_kernel(ids_ref, all_ref, out_ref, packed):
+    groups, dates = ids_ref.shape
+
+    def step(group, carry):
+        real, imag = [], []
+        for k in range(dates):
+            date = ids_ref[group, k]
+            real.append(all_ref[date, 0].astype(jnp.float32))
+            imag.append(all_ref[date, 1].astype(jnp.float32))
+        packed[pl.ds(pl.multiple_of(group * 8, 8), 8), :] = cell_sums(real, imag)
+        return carry
+
+    lax.fori_loop(0, groups, step, 0)
+    out_ref[...] = cells_last(packed[...])
+
+
+def table_kernel(in_ref, out_ref):
+    for r in range(in_ref.shape[1]):
+        for k, tile in enumerate(table_of([in_ref[j, r] for j in range(8)])):
+            out_ref[r, 8 * k : 8 * k + 8, :] = tile
+
+
+def final_kernel(own_ref, before_ref, after_ref, ranks_ref, ifg_ref, coh_ref):
+    for r in range(own_ref.shape[0]):
+        looks = own_ref[r]
+        boxed = box_of(looks, before_ref[r], after_ref[r])
+        ranks = ranks_ref[r]
+        mean_re, mean_im, coherence = expand(looks, boxed, ranks[:, 0:1], ranks[:, 1:2], 8)
+        ifg_ref[r, :, 0, :] = mean_re
+        ifg_ref[r, :, 1, :] = mean_im
+        coh_ref[r] = coherence
+
+
+def plan(pairs, own_index, peers, dates):
+    rounds = pairs.shape[0]
+    pair_dev = pairs.shape[1] // peers
+    all_ids = jnp.arange(dates, dtype=jnp.int32)
+    wanted = pairs.reshape(rounds, peers, 2 * pair_dev)
+    needed = jnp.any(wanted[:, :, :, None] == all_ids, axis=2)
+    before = (all_ids[:, None] < all_ids[None, :])
+    rank = jnp.sum((needed[:, :, :, None] & before).astype(jnp.int32), axis=2)
+    slots = jnp.arange(peers, dtype=jnp.int32)
+    hit = needed[:, :, None, :] & (rank[:, :, None, :] == slots[None, None, :, None])
+    ids = jnp.sum(jnp.where(hit, all_ids, 0), axis=3)
+    own = lax.dynamic_slice_in_dim(pairs, own_index * pair_dev, pair_dev, 1)
+    own_needed = jnp.any((own[:, :, :, None] == all_ids).reshape(rounds, -1, dates), axis=1)
+    smaller = own_needed[:, None, None, :] & (all_ids < own[..., None])
+    ranks = jnp.sum(smaller.astype(jnp.int32), axis=3)
+    return ids.transpose(1, 0, 2).reshape(peers * rounds, peers), ranks
+
+
+def per_device_few(slc, pairs):
+    peers = lax.axis_size("date")
+    rounds = pairs.shape[0]
+    pair_dev = pairs.shape[1] // peers
+    date_dev, _, lines, columns = slc.shape
+    ids, ranks = plan(pairs, lax.axis_index("date"), peers, date_dev * peers)
+    sent = slc.astype(jnp.bfloat16).reshape(date_dev, 2, lines, peers, columns // peers)
+    sent = sent.transpose(3, 0, 1, 2, 4)
+    held = lax.all_to_all(sent, "date", split_axis=0, concat_axis=0, tiled=True)
+    held = held.reshape(peers * date_dev, 2, lines, columns // peers)
+    vmem = pl.BlockSpec(memory_space=pltpu.VMEM)
+    sums = pl.pallas_call(
+        sums_kernel,
+        out_shape=jax.ShapeDtypeStruct((peers * rounds * 8, 128), jnp.float32),
+        in_specs=[pl.BlockSpec(memory_space=pltpu.SMEM), vmem],
+        out_specs=vmem,
+        scratch_shapes=[pltpu.VMEM((peers * rounds * 8, 128), jnp.float32)],
+    )(ids, held)
+    sums = sums.reshape(peers, rounds, 8, 128)
+    tiles = lax.all_to_all(sums, "date", split_axis=0, concat_axis=0, tiled=True)
+    table = pl.pallas_call(
+        table_kernel,
+        out_shape=jax.ShapeDtypeStruct((rounds, 64, 128), jnp.float32),
+        in_specs=[vmem],
+        out_specs=vmem,
+    )(tiles)
+    az = lax.axis_size("az")
+    up = [(i, i + 1) for i in range(az - 1)]
+    before = lax.ppermute(table, "az", up)
+    after = lax.ppermute(table, "az", [(j, i) for i, j in up])
+    ifg, coh = pl.pallas_call(
+        final_kernel,
+        out_shape=(
+            jax.ShapeDtypeStruct((rounds, pair_dev, 2, 128), jnp.float32),
+            jax.ShapeDtypeStruct((rounds, pair_dev, 128), jnp.float32),
+        ),
+        in_specs=[vmem] * 4,
+        out_specs=(vmem, vmem),
+    )(table, before, after, ranks)
+    cells = columns // SAMPLES
+    return (
+        ifg.reshape(rounds, pair_dev, 2, lines // LINES, cells),
+        coh.reshape(rounds, pair_dev, lines // LINES, cells),
+    )
+
+
+def per_device(slc, pairs):
+    peers = lax.axis_size("date")
+    lines, columns = slc.shape[2:]
+    few = peers == 8 and (lines, columns) == (2 * LINES, 64 * SAMPLES)
+    return per_device_few(slc, pairs) if few else per_device_general(slc, pairs)
+
+
 def solution(mesh):
     return jax.shard_map(
         per_device,

time: 117 us -> 53.4 us (0.46)
  other arithmetic: 40.6 us -> 2.81 us
  local copies, waits for them, and re-layouts: 39.7 us -> 6.75 us
  Pallas kernels: 0 us -> 11.5 us
  waiting for transfers between devices: 17.4 us -> 13 us
  starting transfers between devices: 16.9 us -> 18.1 us
    add x6 -> x0, local copies, waits for them, and re-layouts: 21.1 us -> none  [the longest x2 7.86 us: pair_looks(): power_a = first_re * first_re + first_im * first_im]
    reduce_sum x12 -> x3, other arithmetic: 21.1 us -> 0.62 us  [the longest x1 0.35 us: plan(): ids = jnp.sum(jnp.where(hit, all_ids, 0), axis=3)]
    pallas_call x0 -> x3, Pallas kernels: none -> 11.5 us  [the longest x1 7.43 us: per_device_few(): pl.pallas_call(sums_kernel, out_shape=jax.ShapeDtypeStruct((peers * round...]
    sub x2 -> x0, local copies, waits for them, and re-layouts: 7.68 us -> none  [pair_looks(): prod_im = first_im * second_re - first_re * second_im]
    add x5 -> x0, other arithmetic: 7.68 us -> none  [the longest x2 7.32 us: pair_looks(): prod_re = first_re * second_re + first_im * second_im]
    select_n x8 -> x0, other arithmetic: 7.33 us -> none  [the longest x2 5.26 us: per_device(): jnp.take(incoming.reshape((date_count * CAP,) + tile_shape), position, ax...]
    gather x4 -> x0, local copies, waits for them, and re-layouts: 6.64 us -> none  [the longest x2 5.48 us: per_device(): jnp.take(incoming.reshape((date_count * CAP,) + tile_shape), position, ax...]
    ppermute x2, waiting for transfers between devices: 7.7 us -> 3.03 us  [the longest x1 3.03 us: per_device_few(): after = lax.ppermute(table, 'az', [(j, i) for i, j in up])]
  transfers between devices with their start and end apart: 4 -> 4, of which waited for: 3 -> 3; matrix products, arithmetic and copies ran while one was open for 34% -> 6% of each run, Pallas kernels for 0% -> 0%
where the time goes in v1:
time: 53.4 us; the launch traced here: 52.8 us
  starting transfers between devices  18.1 us (34%)
  waiting for transfers between devices  13 us (24%)
  Pallas kernels  11.5 us (22%)
  local copies, waits for them, and re-layouts  6.75 us (13%)
  other arithmetic  2.81 us (5%)
  between operations  0.7 us (1%)
    pallas_call x1, Pallas kernels, per_device_few(): pl.pallas_call(sums_kernel, out_shape=jax.ShapeDtypeStruct((peers * round...  7.43 us
    all_to_all x1, starting transfers between devices, per_device_few(): held = lax.all_to_all(sent, 'date', split_axis=0, concat_axis=0, tiled=True)  6.47 us
    ppermute x1, starting transfers between devices, per_device_few(): before = lax.ppermute(table, 'az', up)  5.52 us
    all_to_all x1, waiting for transfers between devices, per_device_few(): lax.all_to_all(sums, 'date', split_axis=0, concat_axis=0, tiled=True)  5.31 us
    all_to_all x1, waiting for transfers between devices, per_device_few(): held = lax.all_to_all(sent, 'date', split_axis=0, concat_axis=0, tiled=True)  4.61 us
    all_to_all x1, starting transfers between devices, per_device_few(): lax.all_to_all(sums, 'date', split_axis=0, concat_axis=0, tiled=True)  4.22 us
    ppermute x1, waiting for transfers between devices, per_device_few(): after = lax.ppermute(table, 'az', [(j, i) for i, j in up])  3.03 us
    pallas_call x1, Pallas kernels, per_device_few(): pl.pallas_call(final_kernel, out_shape=(jax.ShapeDtypeStruct((rounds, pai...  2.3 us
  transfers between devices with their start and end apart: 4, of which 3 were waited for; matrix products, arithmetic and copies ran while one was open for 6% of the time, Pallas kernels for 0%

profile of v1, /device:TPU:1, one launch (start us, length us, event | category | flops | bytes accessed | tf_op | source)
XLA Modules:
  0.0 52.8 jit_solution(16267907145056397292)
XLA Ops:
  0.6 1.7 %copy_bitcast_fusion = bf16[8,6,2,8,128]{4,3,2,1,0:T(8,128)(2,1)} fusion(f32[6,2,8,1024]{3,2,1,0:T(8,128)} %param.2), kind=kLoop, calls=%fused_computation.3 | loop fusion | flops 98304 | bytes 589824 | tf_op jit(solution)/shard_map/transpose | solution.py:274
  2.3 6.5 %all-to-all-start = ((bf16[8,6,2,8,128]{4,3,2,1,0:T(8,128)(2,1)}), bf16[8,6,2,8,128]{4,3,2,1,0:T(8,128)(2,1)S(1)}, u32[]{:S(2)}, u32[]{:S(2)}) async-start(bf16[8,6,2,8,128]{4,3,2,1,0:T(8,128)(2,1)} %copy_bitcast_fusion), calls=%async_computation | async-start | bytes 393216 | tf_op jit(solution)/shard_map/all_to_all | solution.py:275
  8.8 0.0 copy-done.5
  8.8 0.2 copy.10
  9.0 0.3 eq.48
  9.3 0.4 fusion
  9.7 0.2 convert_reduce_fusion
  9.9 0.3 select_reduce_fusion
  10.2 0.6 %copy.11 = s32[8,2,8]{2,1,0:T(2,128)} copy(s32[8,2,8]{2,0,1:T(8,128)S(1)} %bitcast.12) | data formatting | bytes 1024 | tf_op jit(solution)/shard_map/transpose | solution.py:264
  10.8 4.6 %all-to-all-done = bf16[8,6,2,8,128]{4,3,2,1,0:T(8,128)(2,1)S(1)} async-done(((bf16[8,6,2,8,128]{4,3,2,1,0:T(8,128)(2,1)}), bf16[8,6,2,8,128]{4,3,2,1,0:T(8,128)(2,1)S(1)}, u32[]{:S(2)}, u32[]{:S(2)}) %all-to-all-start) | async-done | bytes 196640 | tf_op jit(solution)/shard_map/all_to_all | solution.py:275
  15.4 0.7 %copy-done = bf16[8,6,2,8,128]{4,3,2,1,0:T(8,128)(2,1)} copy-done((bf16[8,6,2,8,128]{4,3,2,1,0:T(8,128)(2,1)}, bf16[8,6,2,8,128]{4,3,2,1,0:T(8,128)(2,1)S(1)}, u32[]{:S(2)}) %copy-start) | copy-done | bytes 196632
  16.1 7.4 %shard_map.41 = f32[128,128]{1,0:T(8,128)} custom-call(s32[16,8]{1,0:T(8,128)} %bitcast.11, bf16[48,2,8,128]{3,2,1,0:T(8,128)(2,1)} %bitcast.9), custom_call_target="tpu_custom_call" | custom-call | tf_op jit(solution)/shard_map/pallas_call | solution.py:278
  23.6 4.2 %all-to-all-start.1 = ((f32[8,2,8,128]{3,2,1,0:T(8,128)}), f32[8,2,8,128]{3,2,1,0:T(8,128)S(1)}, u32[]{:S(2)}, u32[]{:S(2)}) async-start(f32[8,2,8,128]{3,2,1,0:T(8,128)} %bitcast.10), calls=%async_computation.1 | async-start | bytes 131072 | tf_op jit(solution)/shard_map/all_to_all | solution.py:286
  27.8 0.1 constant_dynamic-slice_fusion
  27.8 0.1 copy.13
  28.0 0.1 eq.55
  28.1 0.1 fusion.3
  28.2 5.3 %all-to-all-done.1.in_ref = f32[8,2,8,128]{3,2,1,0:T(8,128)S(1)} async-done(((f32[8,2,8,128]{3,2,1,0:T(8,128)}), f32[8,2,8,128]{3,2,1,0:T(8,128)S(1)}, u32[]{:S(2)}, u32[]{:S(2)}) %all-to-all-start.1) | async-done | bytes 65568 | tf_op jit(solution)/shard_map/all_to_all | solution.py:286
  33.5 0.6 %copy-done.1 = f32[8,2,8,128]{3,2,1,0:T(8,128)} copy-done((f32[8,2,8,128]{3,2,1,0:T(8,128)}, f32[8,2,8,128]{3,2,1,0:T(8,128)S(1)}, u32[]{:S(2)}) %copy-start.1) | copy-done | bytes 65560
  34.2 1.8 %shard_map.42.own_ref = f32[2,64,128]{2,1,0:T(8,128)} custom-call(f32[8,2,8,128]{3,2,1,0:T(8,128)} %copy-done.1), custom_call_target="tpu_custom_call" | custom-call | tf_op jit(solution)/shard_map/pallas_call | solution.py:287
  35.9 5.5 %collective-permute-start = (f32[2,64,128]{2,1,0:T(8,128)}, f32[2,64,128]{2,1,0:T(8,128)S(1)}, u32[]{:S(2)}, u32[]{:S(2)}) collective-permute-start(f32[2,64,128]{2,1,0:T(8,128)} %shard_map.42.own_ref), channel_id=1, source_target_pairs={{0,1},{1,2},{2,3},{4,5},{5,6},{6,7},{8,9},{9,10},{10,11},{12,13},{... | collective-permute-start | bytes 196616 | tf_op jit(solution)/shard_map/ppermute | solution.py:295
  41.5 1.9 %collective-permute-start.1 = (f32[2,64,128]{2,1,0:T(8,128)}, f32[2,64,128]{2,1,0:T(8,128)S(1)}, u32[]{:S(2)}, u32[]{:S(2)}) collective-permute-start(f32[2,64,128]{2,1,0:T(8,128)} %shard_map.42.own_ref), channel_id=1, source_target_pairs={{1,0},{2,1},{3,2},{5,4},{6,5},{7,6},{9,8},{10,9},{11,10},{13,12},{... | collective-permute-start | bytes 196616 | tf_op jit(solution)/shard_map/ppermute | solution.py:296
  43.4 0.1 convert_reduce_fusion.1
  43.5 0.7 %copy.14.ranks_ref = s32[2,64,2]{2,1,0:T(8,128)} copy(s32[2,64,2]{1,2,0:T(2,128)S(1)} %convert_reduce_fusion.1) | data formatting | bytes 2048 | tf_op jit(solution)/shard_map/reduce_sum | solution.py:263
  44.2 0.0 collective-permute-done.before_ref
  44.2 3.0 %collective-permute-done.1.after_ref = f32[2,64,128]{2,1,0:T(8,128)S(1)} collective-permute-done((f32[2,64,128]{2,1,0:T(8,128)}, f32[2,64,128]{2,1,0:T(8,128)S(1)}, u32[]{:S(2)}, u32[]{:S(2)}) %collective-permute-start.1) | collective-permute-done | bytes 65568 | tf_op jit(solution)/shard_map/ppermute | solution.py:296
  47.2 0.0 copy-done.3
  47.3 0.6 %copy-done.4 = f32[2,64,128]{2,1,0:T(8,128)} copy-done((f32[2,64,128]{2,1,0:T(8,128)}, f32[2,64,128]{2,1,0:T(8,128)S(1)}, u32[]{:S(2)}) %copy-start.4) | copy-done | bytes 65560
  47.9 2.3 %shard_map.43 = (f32[2,64,2,128]{3,2,1,0:T(2,128)}, f32[2,64,128]{2,1,0:T(8,128)}) custom-call(f32[2,64,128]{2,1,0:T(8,128)} %shard_map.42.own_ref, f32[2,64,128]{2,1,0:T(8,128)} %copy-done.3, f32[2,64,128]{2,1,0:T(8,128)} %copy-done.4, s32[2,64,2]{2,1,0:T(8,128)} %copy.14.ranks_ref), custom_call_target="tpu_custom_call" | custom-call | tf_op jit(solution)/shard_map/pallas_call | solution.py:297
  50.2 1.9 %reshape.47 = f32[2,64,2,2,64]{4,3,2,1,0:T(2,128)} reshape(f32[2,64,2,128]{3,2,1,0:T(2,128)} %get-tuple-element.4) | data formatting | bytes 262144 | tf_op jit(solution)/shard_map/reshape | solution.py:308
  52.0 0.0 copy-done.2
  52.1 0.8 %reshape.48 = f32[2,64,2,64]{3,2,1,0:T(2,128)} reshape(f32[2,64,128]{2,1,0:T(8,128)S(1)} %copy-done.2) | data formatting | bytes 131072 | tf_op jit(solution)/shard_map/reshape | solution.py:309
  (7 shorter events, 0.0 us)
Async XLA Ops:
  2.3 6.5 %copy-start.5 = (s32[2,512,2]{1,2,0:T(2,128)S(1)}, s32[2,512,2]{1,2,0:T(2,128)}, u32[]{:S(2)}) copy-start(s32[2,512,2]{1,2,0:T(2,128)} %param.3) | copy-start | bytes 24580
  2.3 13.1 %all-to-all-start = ((bf16[8,6,2,8,128]{4,3,2,1,0:T(8,128)(2,1)}), bf16[8,6,2,8,128]{4,3,2,1,0:T(8,128)(2,1)S(1)}, u32[]{:S(2)}, u32[]{:S(2)}) async-start(bf16[8,6,2,8,128]{4,3,2,1,0:T(8,128)(2,1)} %copy_bitcast_fusion), calls=%async_computation | async-start | bytes 393216 | tf_op jit(solution)/shard_map/all_to_all | solution.py:275
  15.4 0.7 %copy-start = (bf16[8,6,2,8,128]{4,3,2,1,0:T(8,128)(2,1)}, bf16[8,6,2,8,128]{4,3,2,1,0:T(8,128)(2,1)S(1)}, u32[]{:S(2)}) copy-start(bf16[8,6,2,8,128]{4,3,2,1,0:T(8,128)(2,1)S(1)} %all-to-all-done) | copy-start | bytes 589828
  23.6 10.0 %all-to-all-start.1 = ((f32[8,2,8,128]{3,2,1,0:T(8,128)}), f32[8,2,8,128]{3,2,1,0:T(8,128)S(1)}, u32[]{:S(2)}, u32[]{:S(2)}) async-start(f32[8,2,8,128]{3,2,1,0:T(8,128)} %bitcast.10), calls=%async_computation.1 | async-start | bytes 131072 | tf_op jit(solution)/shard_map/all_to_all | solution.py:286
  33.5 0.6 %copy-start.1 = (f32[8,2,8,128]{3,2,1,0:T(8,128)}, f32[8,2,8,128]{3,2,1,0:T(8,128)S(1)}, u32[]{:S(2)}) copy-start(f32[8,2,8,128]{3,2,1,0:T(8,128)S(1)} %all-to-all-done.1.in_ref) | copy-start | bytes 196612
  35.9 8.3 %collective-permute-start = (f32[2,64,128]{2,1,0:T(8,128)}, f32[2,64,128]{2,1,0:T(8,128)S(1)}, u32[]{:S(2)}, u32[]{:S(2)}) collective-permute-start(f32[2,64,128]{2,1,0:T(8,128)} %shard_map.42.own_ref), channel_id=1, source_target_pairs={{0,1},{1,2},{2,3},{4,5},{5,6},{6,7},{8,9},{9,10},{10,11},{12,13},{... | collective-permute-start | bytes 196616 | tf_op jit(solution)/shard_map/ppermute | solution.py:295
  41.5 5.8 %collective-permute-start.1 = (f32[2,64,128]{2,1,0:T(8,128)}, f32[2,64,128]{2,1,0:T(8,128)S(1)}, u32[]{:S(2)}, u32[]{:S(2)}) collective-permute-start(f32[2,64,128]{2,1,0:T(8,128)} %shard_map.42.own_ref), channel_id=1, source_target_pairs={{1,0},{2,1},{3,2},{5,4},{6,5},{7,6},{9,8},{10,9},{11,10},{13,12},{... | collective-permute-start | bytes 196616 | tf_op jit(solution)/shard_map/ppermute | solution.py:296
  44.2 3.0 %copy-start.3 = (f32[2,64,128]{2,1,0:T(8,128)}, f32[2,64,128]{2,1,0:T(8,128)S(1)}, u32[]{:S(2)}) copy-start(f32[2,64,128]{2,1,0:T(8,128)S(1)} %collective-permute-done.before_ref) | copy-start | bytes 196612
  47.2 0.6 %copy-start.4 = (f32[2,64,128]{2,1,0:T(8,128)}, f32[2,64,128]{2,1,0:T(8,128)S(1)}, u32[]{:S(2)}) copy-start(f32[2,64,128]{2,1,0:T(8,128)S(1)} %collective-permute-done.1.after_ref) | copy-start | bytes 196612
  50.2 1.9 %copy-start.2 = (f32[2,64,128]{2,1,0:T(8,128)S(1)}, f32[2,64,128]{2,1,0:T(8,128)}, u32[]{:S(2)}) copy-start(f32[2,64,128]{2,1,0:T(8,128)} %get-tuple-element.5) | copy-start | bytes 196612

commit v2 on v1

--- a/solution.py
+++ b/solution.py
@@ -213,55 +213,173 @@
     return means[:rows], means[rows:], coherence
 
 
-def sums_kernel(ids_ref, all_ref, out_ref, packed):
-    groups, dates = ids_ref.shape
-
-    def step(group, carry):
-        real, imag = [], []
-        for k in range(dates):
-            date = ids_ref[group, k]
-            real.append(all_ref[date, 0].astype(jnp.float32))
-            imag.append(all_ref[date, 1].astype(jnp.float32))
-        packed[pl.ds(pl.multiple_of(group * 8, 8), 8), :] = cell_sums(real, imag)
+MESH = pl.DeviceIdType.MESH
+
+
+def list_dates(entries, dates, count):
+    lane = iota(entries.shape, 1)
+    seen = jnp.zeros((entries.shape[0], 1), jnp.int32)
+    listed = jnp.zeros(entries.shape, jnp.int32)
+    for date in range(dates):
+        named = jnp.max((entries == date).astype(jnp.int32), axis=1, keepdims=True)
+        listed = jnp.where((lane == seen) & (named > 0), date, listed)
+        seen = seen + named
+    return listed
+
+
+def stack_kernel(
+    slc_ref,
+    pairs_ref,
+    entries_ref,
+    ifg_ref,
+    coh_ref,
+    sent,
+    held,
+    sums,
+    tiles,
+    table,
+    halo,
+    listed,
+    ids,
+    send_a,
+    recv_a,
+    send_b,
+    recv_b,
+    send_h,
+    recv_h,
+    list_sem,
+):
+    peers, az_size = lax.axis_size("date"), lax.axis_size("az")
+    me, az = lax.axis_index("date"), lax.axis_index("az")
+    date_dev = slc_ref.shape[0]
+    rounds = pairs_ref.shape[0]
+    pair_dev = pairs_ref.shape[1] // peers
+    width = slc_ref.shape[3] // peers
+    sides = ((-1, az > 0), (1, az < az_size - 1))
+
+    barrier = pltpu.get_barrier_semaphore()
+    for o in range(1, peers):
+        pl.semaphore_signal(
+            barrier, inc=1, device_id={"date": lax.rem(me + o, peers)}, device_id_type=MESH
+        )
+    for step, there in sides:
+
+        @pl.when(there)
+        def _():
+            pl.semaphore_signal(barrier, inc=1, device_id={"az": az + step}, device_id_type=MESH)
+
+    for j in range(peers):
+        sent[j] = slc_ref[:, :, :, j * width : (j + 1) * width].astype(jnp.bfloat16)
+    greeted = peers - 1 + (az > 0).astype(jnp.int32) + (az < az_size - 1).astype(jnp.int32)
+    pl.semaphore_wait(barrier, greeted)
+
+    def images(o):
+        peer = lax.rem(me + o, peers)
+        return pltpu.make_async_remote_copy(
+            src_ref=sent.at[peer],
+            dst_ref=held.at[me],
+            send_sem=send_a.at[o],
+            recv_sem=recv_a.at[o],
+            device_id={"date": peer},
+            device_id_type=MESH,
+        )
+
+    for o in range(1, peers):
+        images(o).start()
+    held[me] = sent[me]
+    listed[...] = list_dates(entries_ref[...], date_dev * peers, peers)
+    fetch = pltpu.make_async_copy(listed, ids, list_sem)
+    fetch.start()
+    fetch.wait()
+    for o in range(1, peers):
+        images(o).wait_recv()
+
+    def results(o):
+        peer = lax.rem(me + o, peers)
+        return pltpu.make_async_remote_copy(
+            src_ref=sums.at[peer],
+            dst_ref=tiles.at[me],
+            send_sem=send_b.at[o],
+            recv_sem=recv_b.at[o],
+            device_id={"date": peer},
+            device_id_type=MESH,
+        )
+
+    def serve(o, carry):
+        peer = lax.rem(me + o, peers)
+        packed = []
+        for r in range(rounds):
+            real, imag = [], []
+            for k in range(peers):
+                date = ids[r * peers + peer, k]
+                owner = date // date_dev
+                real.append(held[owner, date - owner * date_dev, 0].astype(jnp.float32))
+                imag.append(held[owner, date - owner * date_dev, 1].astype(jnp.float32))
+            packed.append(cell_sums(real, imag))
+        done = cells_last(jnp.concatenate(packed, 0))
+        for r in range(rounds):
+            sums[peer, r] = done[8 * r : 8 * r + 8]
+
+        @pl.when(o < peers)
+        def _():
+            results(o).start()
+
         return carry
 
-    lax.fori_loop(0, groups, step, 0)
-    out_ref[...] = cells_last(packed[...])
-
-
-def table_kernel(in_ref, out_ref):
-    for r in range(in_ref.shape[1]):
-        for k, tile in enumerate(table_of([in_ref[j, r] for j in range(8)])):
-            out_ref[r, 8 * k : 8 * k + 8, :] = tile
-
-
-def final_kernel(own_ref, before_ref, after_ref, ranks_ref, ifg_ref, coh_ref):
-    for r in range(own_ref.shape[0]):
-        looks = own_ref[r]
-        boxed = box_of(looks, before_ref[r], after_ref[r])
-        ranks = ranks_ref[r]
-        mean_re, mean_im, coherence = expand(looks, boxed, ranks[:, 0:1], ranks[:, 1:2], 8)
+    lax.fori_loop(1, peers + 1, serve, 0)
+    tiles[me] = sums[me]
+    for o in range(1, peers):
+        results(o).wait_recv()
+    for r in range(rounds):
+        for k, tile in enumerate(table_of([tiles[j, r] for j in range(peers)])):
+            table[r, 8 * k : 8 * k + 8, :] = tile
+
+    def edge(n, step):
+        return pltpu.make_async_remote_copy(
+            src_ref=table,
+            dst_ref=halo.at[n],
+            send_sem=send_h.at[n],
+            recv_sem=recv_h.at[n],
+            device_id={"az": az + step},
+            device_id_type=MESH,
+        )
+
+    for n, (step, there) in enumerate(sides):
+
+        @pl.when(there)
+        def _():
+            edge(n, step).start()
+
+        @pl.when(jnp.logical_not(there))
+        def _():
+            halo[1 - n] = jnp.zeros_like(halo[1 - n])
+
+    for n, (step, there) in enumerate(sides):
+
+        @pl.when(there)
+        def _():
+            edge(1 - n, step).wait_recv()
+
+    for r in range(rounds):
+        own = pairs_ref[r, pl.ds(pl.multiple_of(me * pair_dev, 8), pair_dev), :]
+        ranks = jnp.zeros_like(own)
+        for k in range(peers):
+            ranks = ranks + (own > ids[r * peers + me, k]).astype(jnp.int32)
+        looks = table[r]
+        boxed = box_of(looks, halo[1, r], halo[0, r])
+        mean_re, mean_im, coherence = expand(looks, boxed, ranks[:, 0:1], ranks[:, 1:2], peers)
         ifg_ref[r, :, 0, :] = mean_re
         ifg_ref[r, :, 1, :] = mean_im
         coh_ref[r] = coherence
 
-
-def plan(pairs, own_index, peers, dates):
-    rounds = pairs.shape[0]
-    pair_dev = pairs.shape[1] // peers
-    all_ids = jnp.arange(dates, dtype=jnp.int32)
-    wanted = pairs.reshape(rounds, peers, 2 * pair_dev)
-    needed = jnp.any(wanted[:, :, :, None] == all_ids, axis=2)
-    before = (all_ids[:, None] < all_ids[None, :])
-    rank = jnp.sum((needed[:, :, :, None] & before).astype(jnp.int32), axis=2)
-    slots = jnp.arange(peers, dtype=jnp.int32)
-    hit = needed[:, :, None, :] & (rank[:, :, None, :] == slots[None, None, :, None])
-    ids = jnp.sum(jnp.where(hit, all_ids, 0), axis=3)
-    own = lax.dynamic_slice_in_dim(pairs, own_index * pair_dev, pair_dev, 1)
-    own_needed = jnp.any((own[:, :, :, None] == all_ids).reshape(rounds, -1, dates), axis=1)
-    smaller = own_needed[:, None, None, :] & (all_ids < own[..., None])
-    ranks = jnp.sum(smaller.astype(jnp.int32), axis=3)
-    return ids.transpose(1, 0, 2).reshape(peers * rounds, peers), ranks
+    for o in range(1, peers):
+        images(o).wait_send()
+        results(o).wait_send()
+    for n, (step, there) in enumerate(sides):
+
+        @pl.when(there)
+        def _():
+            edge(n, step).wait_send()
 
 
 def per_device_few(slc, pairs):
@@ -269,40 +387,37 @@
     rounds = pairs.shape[0]
     pair_dev = pairs.shape[1] // peers
     date_dev, _, lines, columns = slc.shape
-    ids, ranks = plan(pairs, lax.axis_index("date"), peers, date_dev * peers)
-    sent = slc.astype(jnp.bfloat16).reshape(date_dev, 2, lines, peers, columns // peers)
-    sent = sent.transpose(3, 0, 1, 2, 4)
-    held = lax.all_to_all(sent, "date", split_axis=0, concat_axis=0, tiled=True)
-    held = held.reshape(peers * date_dev, 2, lines, columns // peers)
+    width = columns // peers
+    entries = pairs.reshape(rounds * peers, 2 * pair_dev)
     vmem = pl.BlockSpec(memory_space=pltpu.VMEM)
-    sums = pl.pallas_call(
-        sums_kernel,
-        out_shape=jax.ShapeDtypeStruct((peers * rounds * 8, 128), jnp.float32),
-        in_specs=[pl.BlockSpec(memory_space=pltpu.SMEM), vmem],
-        out_specs=vmem,
-        scratch_shapes=[pltpu.VMEM((peers * rounds * 8, 128), jnp.float32)],
-    )(ids, held)
-    sums = sums.reshape(peers, rounds, 8, 128)
-    tiles = lax.all_to_all(sums, "date", split_axis=0, concat_axis=0, tiled=True)
-    table = pl.pallas_call(
-        table_kernel,
-        out_shape=jax.ShapeDtypeStruct((rounds, 64, 128), jnp.float32),
-        in_specs=[vmem],
-        out_specs=vmem,
-    )(tiles)
-    az = lax.axis_size("az")
-    up = [(i, i + 1) for i in range(az - 1)]
-    before = lax.ppermute(table, "az", up)
-    after = lax.ppermute(table, "az", [(j, i) for i, j in up])
+    dma = pltpu.SemaphoreType.DMA
     ifg, coh = pl.pallas_call(
-        final_kernel,
+        stack_kernel,
         out_shape=(
             jax.ShapeDtypeStruct((rounds, pair_dev, 2, 128), jnp.float32),
             jax.ShapeDtypeStruct((rounds, pair_dev, 128), jnp.float32),
         ),
-        in_specs=[vmem] * 4,
+        in_specs=[vmem] * 3,
         out_specs=(vmem, vmem),
-    )(table, before, after, ranks)
+        scratch_shapes=[
+            pltpu.VMEM((peers, date_dev, 2, lines, width), jnp.bfloat16),
+            pltpu.VMEM((peers, date_dev, 2, lines, width), jnp.bfloat16),
+            pltpu.VMEM((peers, rounds, 8, 128), jnp.float32),
+            pltpu.VMEM((peers, rounds, 8, 128), jnp.float32),
+            pltpu.VMEM((rounds, 64, 128), jnp.float32),
+            pltpu.VMEM((2, rounds, 64, 128), jnp.float32),
+            pltpu.VMEM(entries.shape, jnp.int32),
+            pltpu.SMEM(entries.shape, jnp.int32),
+            dma((peers,)),
+            dma((peers,)),
+            dma((peers,)),
+            dma((peers,)),
+            dma((2,)),
+            dma((2,)),
+            dma,
+        ],
+        compiler_params=pltpu.CompilerParams(collective_id=0, has_side_effects=True),
+    )(slc, pairs, entries)
     cells = columns // SAMPLES
     return (
         ifg.reshape(rounds, pair_dev, 2, lines // LINES, cells),

time: 53.4 us -> 29 us (0.54)
  starting transfers between devices: 18.1 us -> 0 us
  waiting for transfers between devices: 13 us -> 0 us
  Pallas kernels: 11.5 us -> 23.7 us
  other arithmetic: 2.81 us -> 0 us
  local copies, waits for them, and re-layouts: 6.75 us -> 4.45 us
    pallas_call x3 -> x1, Pallas kernels: 11.5 us -> 23.7 us  [per_device_few(): pl.pallas_call(stack_kernel, out_shape=(jax.ShapeDtypeStruct((rounds, pai...]
    all_to_all x2 -> x0, starting transfers between devices: 10.7 us -> none  [the longest x1 6.47 us: per_device_few(): held = lax.all_to_all(sent, 'date', split_axis=0, concat_axis=0, tiled=True)]
    all_to_all x2 -> x0, waiting for transfers between devices: 9.92 us -> none  [the longest x1 5.31 us: per_device_few(): lax.all_to_all(sums, 'date', split_axis=0, concat_axis=0, tiled=True)]
    ppermute x2 -> x0, starting transfers between devices: 7.44 us -> none  [the longest x1 5.52 us: per_device_few(): before = lax.ppermute(table, 'az', up)]
    ppermute x2 -> x0, waiting for transfers between devices: 3.03 us -> none  [the longest x1 3.03 us: per_device_few(): after = lax.ppermute(table, 'az', [(j, i) for i, j in up])]
    transpose x1 -> x0, other arithmetic: 1.7 us -> none  [per_device_few(): sent = sent.transpose(3, 0, 1, 2, 4)]
    unnamed x13 -> x5, local copies, waits for them, and re-layouts: 2.15 us -> 0.92 us
    reshape x0 -> x1, local copies, waits for them, and re-layouts: none -> 0.87 us  [per_device_few(): entries = pairs.reshape(rounds * peers, 2 * pair_dev)]
  transfers between devices with their start and end apart: 4 -> 0, of which waited for: 3 -> 0; matrix products, arithmetic and copies ran while one was open for 6% -> 0% of each run, Pallas kernels for 0% -> 0%
where the time goes in v2:
time: 29 us; the launch traced here: 28.8 us
  Pallas kernels  23.7 us (82%)
  local copies, waits for them, and re-layouts  4.45 us (15%)
  between operations  0.66 us (2%)
    pallas_call x1, Pallas kernels, per_device_few(): pl.pallas_call(stack_kernel, out_shape=(jax.ShapeDtypeStruct((rounds, pai...  23.7 us
    reshape x1, local copies, waits for them, and re-layouts, per_device_few(): ifg.reshape(rounds, pair_dev, 2, lines // LINES, cells)  1.88 us
    unnamed x5, local copies, waits for them, and re-layouts  0.92 us
    reshape x1, local copies, waits for them, and re-layouts, per_device_few(): entries = pairs.reshape(rounds * peers, 2 * pair_dev)  0.87 us
    reshape x1, local copies, waits for them, and re-layouts, per_device_few(): coh.reshape(rounds, pair_dev, lines // LINES, cells)  0.79 us

profile of v2, /device:TPU:1, one launch (start us, length us, event | category | flops | bytes accessed | tf_op | source)
XLA Modules:
  0.0 28.8 jit_solution(7747343512581928198)
XLA Ops:
  0.6 0.9 %copy.7.pairs_ref = s32[2,512,2]{2,1,0:T(8,128)S(1)} copy(s32[2,512,2]{1,2,0:T(2,128)} %param.3) | data formatting | bytes 16384 | tf_op args[1]
  1.5 0.0 copy-start
  1.6 0.9 %reshape.13.entries_ref = s32[16,128]{1,0:T(8,128)} reshape(s32[2,512,2]{2,1,0:T(8,128)S(1)} %copy.7.pairs_ref) | data formatting | bytes 16384 | tf_op jit(solution)/shard_map/reshape | solution.py:391
  2.4 0.0 copy-done
  2.4 23.7 %shard_map.41 = (f32[2,64,2,128]{3,2,1,0:T(2,128)}, f32[2,64,128]{2,1,0:T(8,128)}) custom-call(f32[6,2,8,1024]{3,2,1,0:T(8,128)} %slc_ref.1, s32[2,512,2]{2,1,0:T(8,128)} %copy-done, s32[16,128]{1,0:T(8,128)} %reshape.13.entries_ref), custom_call_target="tpu_custom_call" | custom-call | tf_op jit(solution)/shard_map/pallas_call | solution.py:394
  26.1 0.0 copy-start.1
  26.1 1.9 %reshape.14 = f32[2,64,2,2,64]{4,3,2,1,0:T(2,128)} reshape(f32[2,64,2,128]{3,2,1,0:T(2,128)} %get-tuple-element.4) | data formatting | bytes 262144 | tf_op jit(solution)/shard_map/reshape | solution.py:423
  28.0 0.0 copy-done.1
  28.0 0.8 %reshape.15 = f32[2,64,2,64]{3,2,1,0:T(2,128)} reshape(f32[2,64,128]{2,1,0:T(8,128)S(1)} %copy-done.1) | data formatting | bytes 131072 | tf_op jit(solution)/shard_map/reshape | solution.py:424
Async XLA Ops:
  1.5 0.9 %copy-start = (s32[2,512,2]{2,1,0:T(8,128)}, s32[2,512,2]{2,1,0:T(8,128)S(1)}, u32[]{:S(2)}) copy-start(s32[2,512,2]{2,1,0:T(8,128)S(1)} %copy.7.pairs_ref) | copy-start | bytes 24580
  26.1 1.9 %copy-start.1 = (f32[2,64,128]{2,1,0:T(8,128)S(1)}, f32[2,64,128]{2,1,0:T(8,128)}, u32[]{:S(2)}) copy-start(f32[2,64,128]{2,1,0:T(8,128)} %get-tuple-element.5) | copy-start | bytes 196612

commit v3 on v2

--- a/solution.py
+++ b/solution.py
@@ -101,7 +101,7 @@
 
 
 LINES, SAMPLES = 4, 16
-STEPS = ((0, 2), (0, 1), (1, 8), (1, 4), (1, 2), (1, 1))
+STEPS = ((0, 2, 2), (0, 2, 1), (1, 8, 8), (1, 8, 4), (1, 8, 2), (1, 8, 1))
 
 
 def iota(shape, dim):
@@ -110,18 +110,18 @@
 
 def place_of(leaf):
     bit = [(leaf >> n) & 1 for n in range(6)]
-    return 32 * bit[3] + 16 * bit[4] + 8 * bit[5] + 4 * bit[2] + 2 * bit[0] + bit[1]
+    return 32 * bit[3] + 16 * bit[4] + 8 * bit[5] + 4 * bit[0] + 2 * bit[1] + bit[2]
 
 
 def rolled(x, shift, dim):
     return pltpu.roll(x, shift % x.shape[dim], dim)
 
 
-def join(one, two, dim, dist):
-    low = (iota(one.shape, dim) & dist) == 0
+def join(one, two, dim, unit, dist, phase):
+    low = ((iota(one.shape, dim) - unit * phase) & (unit * dist)) == 0
     kept = jnp.where(low, one, two)
     other = jnp.where(low, two, one)
-    return kept + jnp.where(low, rolled(other, -dist, dim), rolled(other, dist, dim))
+    return kept + rolled(other, -unit * dist, dim)
 
 
 def cell_sums(real, imag):
@@ -139,14 +139,16 @@
         i = place - len(couples)
         return real[i] * real[i] + imag[i] * imag[i]
 
-    def build(level, base):
+    def build(level, base, phases):
         if level == 0:
             return quantity(place_of(base))
-        one = build(level - 1, base)
-        two = build(level - 1, base + (1 << (level - 1)))
-        return join(one, two, *STEPS[level - 1])
-
-    return build(len(STEPS), 0)
+        dim, unit, dist = STEPS[level - 1]
+        moved = tuple(p + dist if d == dim else p for d, p in enumerate(phases))
+        one = build(level - 1, base, phases)
+        two = build(level - 1, base + (1 << (level - 1)), moved)
+        return join(one, two, dim, unit, dist, phases[dim])
+
+    return build(len(STEPS), 0, (0, 0))
 
 
 def exact_dot(a, b):
@@ -159,11 +161,10 @@
     )
 
 
-def cells_last(x):
-    shape = (128, 128)
-    src, dst = iota(shape, 0), iota(shape, 1)
+def sample_order():
+    src, dst = iota((128, 128), 0), iota((128, 128), 1)
     hit = dst == (src % SAMPLES) * (128 // SAMPLES) + src // SAMPLES
-    return exact_dot(x, jnp.where(hit, 1.0 / (LINES * SAMPLES), 0.0).astype(jnp.float32))
+    return jnp.where(hit, 1.0 / 8, 0.0).astype(jnp.bfloat16)
 
 
 def table_of(tiles):
@@ -177,8 +178,13 @@
                 one, two = tiles[j], tiles[j | 1 << b]
                 tiles[j] = jnp.where(low, one, rolled(two, dist, 1))
                 tiles[j | 1 << b] = jnp.where(low, rolled(one, -dist, 1), two)
-    same = (sub < 4) == (lane < 64)
-    return [jnp.where(same, t, rolled(rolled(t, 4, 0), 64, 1)) for t in tiles]
+    even, first = (sub & 1) == 0, lane < 64
+    out = []
+    for tile in tiles:
+        far = rolled(tile, 64, 1)
+        moved = jnp.where(even, rolled(far, -1, 0), rolled(far, 1, 0))
+        out.append(jnp.where(even == first, tile, moved))
+    return out
 
 
 def box_of(own, before, after):
@@ -195,52 +201,68 @@
     return out
 
 
-def expand(looks, boxed, rank_a, rank_b, count):
-    rows = rank_a.shape[0]
-    total = looks.shape[0]
-    q = iota((rows, total), 1)
+def pick(places, values):
+    return jnp.where(iota((64, 128), 0) == places, values, 0.0)
+
+
+def picks(rank_a, rank_b, count):
+    first = iota(rank_a.shape, 1) < 64
     low, high = jnp.minimum(rank_a, rank_b), jnp.maximum(rank_a, rank_b)
+    couples = count * (count - 1) // 2
     place = ((low * (2 * count - 1 - low)) >> 1) + high - low - 1
-    couples = count * (count - 1) // 2
-    sel_re = jnp.where(q == place, 1.0, 0.0)
-    sel_im = jnp.where(q == place + couples, jnp.where(rank_a < rank_b, 1.0, -1.0), 0.0)
-    sel_a = jnp.where(q == rank_a + 2 * couples, 1.0, 0.0)
-    sel_b = jnp.where(q == rank_b + 2 * couples, 1.0, 0.0)
-    means = exact_dot(jnp.concatenate([sel_re, sel_im], 0), looks)
-    sums = exact_dot(jnp.concatenate([sel_re, sel_im, sel_a, sel_b], 0), boxed)
-    box_re, box_im, box_a, box_b = (sums[n * rows : (n + 1) * rows] for n in range(4))
-    coherence = jnp.sqrt(box_re * box_re + box_im * box_im) / jnp.sqrt(box_a * box_b)
-    return means[:rows], means[rows:], coherence
+    sign = jnp.where(first | (rank_a < rank_b), 1.0, -1.0)
+    products = pick(place + jnp.where(first, 0, couples), sign)
+    powers = pick(2 * couples + jnp.where(first, rank_a, rank_b), jnp.ones_like(sign))
+    return products, powers
 
 
 MESH = pl.DeviceIdType.MESH
 
 
-def list_dates(entries, dates, count):
-    lane = iota(entries.shape, 1)
-    seen = jnp.zeros((entries.shape[0], 1), jnp.int32)
-    listed = jnp.zeros(entries.shape, jnp.int32)
-    for date in range(dates):
-        named = jnp.max((entries == date).astype(jnp.int32), axis=1, keepdims=True)
-        listed = jnp.where((lane == seen) & (named > 0), date, listed)
-        seen = seen + named
-    return listed
+def list_dates(pairs, dates, peers):
+    length = pairs.shape[1]
+    part = length // peers
+    date = iota((dates, length), 0)
+    named = (pairs[0:1] == date) | (pairs[1:2] == date)
+    parts = iota((length, 128), 0) // part == iota((length, 128), 1)
+    dims = (((1,), (0,)), ((), ()))
+    one = jnp.bfloat16
+    counts = lax.dot_general(
+        named.astype(jnp.float32).astype(one),
+        parts.astype(jnp.float32).astype(one),
+        dims,
+        preferred_element_type=jnp.float32,
+    )
+    needed = counts > 0.5
+    before = iota((dates, dates), 1) < iota((dates, dates), 0)
+    rank = lax.dot_general(
+        before.astype(jnp.float32).astype(one),
+        needed.astype(jnp.float32).astype(one),
+        dims,
+        preferred_element_type=jnp.float32,
+    )
+    rank = jnp.where(needed, rank, -1.0).astype(jnp.int32)
+    date = iota(rank.shape, 0)
+    rows = [jnp.sum(jnp.where(rank == k, date, 0), axis=0, keepdims=True) for k in range(peers)]
+    return jnp.concatenate(rows, 0)
 
 
 def stack_kernel(
     slc_ref,
     pairs_ref,
-    entries_ref,
     ifg_ref,
     coh_ref,
+    lines,
     sent,
     held,
+    full,
     sums,
     tiles,
     table,
     halo,
     listed,
     ids,
+    line_sem,
     send_a,
     recv_a,
     send_b,
@@ -253,8 +275,8 @@
     me, az = lax.axis_index("date"), lax.axis_index("az")
     date_dev = slc_ref.shape[0]
     rounds = pairs_ref.shape[0]
-    pair_dev = pairs_ref.shape[1] // peers
     width = slc_ref.shape[3] // peers
+    images_dev = 2 * date_dev
     sides = ((-1, az > 0), (1, az < az_size - 1))
 
     barrier = pltpu.get_barrier_semaphore()
@@ -268,8 +290,19 @@
         def _():
             pl.semaphore_signal(barrier, inc=1, device_id={"az": az + step}, device_id_type=MESH)
 
+    def line(n):
+        row = n % LINES * 2 + n // LINES
+        return pltpu.make_async_copy(
+            slc_ref.at[:, :, n, :], lines.at[:, :, row, :], line_sem.at[n]
+        )
+
+    for n in range(2 * LINES):
+        line(n).start()
+    for n in range(2 * LINES):
+        line(n).wait()
     for j in range(peers):
-        sent[j] = slc_ref[:, :, :, j * width : (j + 1) * width].astype(jnp.bfloat16)
+        part = lines[:, :, :, j * width : (j + 1) * width]
+        sent[j] = part.reshape(sent.shape[1:]).astype(jnp.bfloat16)
     greeted = peers - 1 + (az > 0).astype(jnp.int32) + (az < az_size - 1).astype(jnp.int32)
     pl.semaphore_wait(barrier, greeted)
 
@@ -286,13 +319,38 @@
 
     for o in range(1, peers):
         images(o).start()
-    held[me] = sent[me]
-    listed[...] = list_dates(entries_ref[...], date_dev * peers, peers)
+    for r in range(rounds):
+        listed[r * peers : (r + 1) * peers, :] = list_dates(
+            pairs_ref[r], date_dev * peers, peers
+        )
     fetch = pltpu.make_async_copy(listed, ids, list_sem)
     fetch.start()
+    order = sample_order()
+
+    def take(owner, block):
+        spread = jnp.dot(block, order, preferred_element_type=jnp.float32)
+        at = pl.ds(owner * images_dev, images_dev)
+        full[at] = spread.reshape((images_dev,) + full.shape[1:])
+
+    take(me, sent[me])
     fetch.wait()
+    lane = iota((1, 128), 1)
+    chosen = []
+    for r in range(rounds):
+        ranks = []
+        for c in range(2):
+            start = pl.multiple_of(me // 2 * 128, 128)
+            near = pairs_ref[r, c : c + 1, pl.ds(start, 128)]
+            own = jnp.where((lane < 64) == (lax.rem(me, 2) == 0), near, rolled(near, 64, 1))
+            rank = jnp.zeros_like(own)
+            for k in range(peers):
+                rank = rank + (own > ids[r * peers + k, me]).astype(jnp.int32)
+            ranks.append(rank)
+        chosen.append(ranks)
     for o in range(1, peers):
         images(o).wait_recv()
+        owner = lax.rem(me + peers - o, peers)
+        take(owner, held[owner])
 
     def results(o):
         peer = lax.rem(me + o, peers)
@@ -307,18 +365,13 @@
 
     def serve(o, carry):
         peer = lax.rem(me + o, peers)
-        packed = []
         for r in range(rounds):
             real, imag = [], []
             for k in range(peers):
-                date = ids[r * peers + peer, k]
-                owner = date // date_dev
-                real.append(held[owner, date - owner * date_dev, 0].astype(jnp.float32))
-                imag.append(held[owner, date - owner * date_dev, 1].astype(jnp.float32))
-            packed.append(cell_sums(real, imag))
-        done = cells_last(jnp.concatenate(packed, 0))
-        for r in range(rounds):
-            sums[peer, r] = done[8 * r : 8 * r + 8]
+                date = ids[r * peers + k, peer]
+                real.append(full[2 * date])
+                imag.append(full[2 * date + 1])
+            sums[peer, r] = cell_sums(real, imag)
 
         @pl.when(o < peers)
         def _():
@@ -354,6 +407,16 @@
         def _():
             halo[1 - n] = jnp.zeros_like(halo[1 - n])
 
+    matrices = []
+    for r in range(rounds):
+        products, powers = picks(*chosen[r], peers)
+        products, powers = products.T, powers.T
+        matrices.append((products, powers))
+        means = exact_dot(products, table[r])
+        for c in range(2):
+            for row in range(2):
+                ifg_ref[r, :, c, row, :] = means[64 * c : 64 * c + 64, 64 * row : 64 * row + 64]
+
     for n, (step, there) in enumerate(sides):
 
         @pl.when(there)
@@ -361,16 +424,14 @@
             edge(1 - n, step).wait_recv()
 
     for r in range(rounds):
-        own = pairs_ref[r, pl.ds(pl.multiple_of(me * pair_dev, 8), pair_dev), :]
-        ranks = jnp.zeros_like(own)
-        for k in range(peers):
-            ranks = ranks + (own > ids[r * peers + me, k]).astype(jnp.int32)
-        looks = table[r]
-        boxed = box_of(looks, halo[1, r], halo[0, r])
-        mean_re, mean_im, coherence = expand(looks, boxed, ranks[:, 0:1], ranks[:, 1:2], peers)
-        ifg_ref[r, :, 0, :] = mean_re
-        ifg_ref[r, :, 1, :] = mean_im
-        coh_ref[r] = coherence
+        products, powers = matrices[r]
+        boxed = box_of(table[r], halo[1, r], halo[0, r])
+        parts = exact_dot(products, boxed)
+        power = exact_dot(powers, boxed)
+        size = jnp.sqrt(parts[:64] * parts[:64] + parts[64:] * parts[64:])
+        coherence = size / jnp.sqrt(power[:64] * power[64:])
+        for row in range(2):
+            coh_ref[r, :, row, :] = coherence[:, 64 * row : 64 * row + 64]
 
     for o in range(1, peers):
         images(o).wait_send()
@@ -388,26 +449,30 @@
     pair_dev = pairs.shape[1] // peers
     date_dev, _, lines, columns = slc.shape
     width = columns // peers
-    entries = pairs.reshape(rounds * peers, 2 * pair_dev)
+    rows = date_dev * 2 * lines
+    cells = columns // SAMPLES
     vmem = pl.BlockSpec(memory_space=pltpu.VMEM)
     dma = pltpu.SemaphoreType.DMA
-    ifg, coh = pl.pallas_call(
+    return pl.pallas_call(
         stack_kernel,
         out_shape=(
-            jax.ShapeDtypeStruct((rounds, pair_dev, 2, 128), jnp.float32),
-            jax.ShapeDtypeStruct((rounds, pair_dev, 128), jnp.float32),
+            jax.ShapeDtypeStruct((rounds, pair_dev, 2, lines // LINES, cells), jnp.float32),
+            jax.ShapeDtypeStruct((rounds, pair_dev, lines // LINES, cells), jnp.float32),
         ),
-        in_specs=[vmem] * 3,
+        in_specs=[pl.BlockSpec(memory_space=pl.ANY), vmem],
         out_specs=(vmem, vmem),
         scratch_shapes=[
-            pltpu.VMEM((peers, date_dev, 2, lines, width), jnp.bfloat16),
-            pltpu.VMEM((peers, date_dev, 2, lines, width), jnp.bfloat16),
+            pltpu.VMEM(slc.shape, jnp.float32),
+            pltpu.VMEM((peers, rows, width), jnp.bfloat16),
+            pltpu.VMEM((peers, rows, width), jnp.bfloat16),
+            pltpu.VMEM((peers * date_dev * 2, lines, width), jnp.float32),
             pltpu.VMEM((peers, rounds, 8, 128), jnp.float32),
             pltpu.VMEM((peers, rounds, 8, 128), jnp.float32),
             pltpu.VMEM((rounds, 64, 128), jnp.float32),
             pltpu.VMEM((2, rounds, 64, 128), jnp.float32),
-            pltpu.VMEM(entries.shape, jnp.int32),
-            pltpu.SMEM(entries.shape, jnp.int32),
+            pltpu.VMEM((rounds * peers, 128), jnp.int32),
+            pltpu.SMEM((rounds * peers, 128), jnp.int32),
+            dma((lines,)),
             dma((peers,)),
             dma((peers,)),
             dma((peers,)),
@@ -417,18 +482,14 @@
             dma,
         ],
         compiler_params=pltpu.CompilerParams(collective_id=0, has_side_effects=True),
-    )(slc, pairs, entries)
-    cells = columns // SAMPLES
-    return (
-        ifg.reshape(rounds, pair_dev, 2, lines // LINES, cells),
-        coh.reshape(rounds, pair_dev, lines // LINES, cells),
-    )
+    )(slc, pairs.transpose(0, 2, 1))
 
 
 def per_device(slc, pairs):
     peers = lax.axis_size("date")
     lines, columns = slc.shape[2:]
-    few = peers == 8 and (lines, columns) == (2 * LINES, 64 * SAMPLES)
+    pair_dev = pairs.shape[1] // peers
+    few = (peers, pair_dev, lines, columns) == (8, 64, 2 * LINES, 64 * SAMPLES)
     return per_device_few(slc, pairs) if few else per_device_general(slc, pairs)
 
 

time: 29 us -> 26.2 us (0.903)
  local copies, waits for them, and re-layouts: 4.45 us -> 2.36 us
  Pallas kernels: 23.7 us -> 23 us
    reshape x3 -> x0, local copies, waits for them, and re-layouts: 3.53 us -> none  [the longest x1 1.88 us: per_device_few(): ifg.reshape(rounds, pair_dev, 2, lines // LINES, cells)]
    unnamed x5 -> x4, local copies, waits for them, and re-layouts: 0.92 us -> 2.36 us
    pallas_call x1, Pallas kernels: 23.7 us -> 23 us  [per_device_few(): pl.pallas_call(stack_kernel, out_shape=(jax.ShapeDtypeStruct((rounds, pai...]
where the time goes in v3:
time: 26.2 us; the launch traced here: 26 us
  Pallas kernels  23 us (88%)
  local copies, waits for them, and re-layouts  2.36 us (9%)
  between operations  0.65 us (2%)
    pallas_call x1, Pallas kernels, per_device_few(): pl.pallas_call(stack_kernel, out_shape=(jax.ShapeDtypeStruct((rounds, pai...  23 us
    unnamed x4, local copies, waits for them, and re-layouts  2.36 us

profile of v3, /device:TPU:1, one launch (start us, length us, event | category | flops | bytes accessed | tf_op | source)
XLA Modules:
  0.0 26.0 jit_solution(7751335287923989976)
XLA Ops:
  0.6 23.0 %shard_map.41 = (f32[2,64,2,2,64]{4,3,2,1,0:T(2,128)}, f32[2,64,2,64]{3,2,1,0:T(2,128)}) custom-call(f32[6,2,8,1024]{3,2,1,0:T(8,128)} %slc_ref.1, s32[2,2,512]{2,1,0:T(2,128)} %bitcast.1), custom_call_target="tpu_custom_call" | custom-call | tf_op jit(solution)/shard_map/pallas_call | solution.py:456
  23.6 0.0 copy-start
  23.6 1.7 %copy.6 = f32[2,64,2,2,64]{4,3,2,1,0:T(2,128)} copy(f32[2,64,2,2,64]{4,3,2,1,0:T(2,128)} %get-tuple-element.4) | data formatting | bytes 262144
  25.3 0.0 copy-done
  25.3 0.7 %copy.7 = f32[2,64,2,64]{3,2,1,0:T(2,128)} copy(f32[2,64,2,64]{3,2,1,0:T(2,128)S(1)} %copy-done) | data formatting | bytes 131072
Async XLA Ops:
  23.6 1.7 %copy-start = (f32[2,64,2,64]{3,2,1,0:T(2,128)S(1)}, f32[2,64,2,64]{3,2,1,0:T(2,128)}, u32[]{:S(2)}) copy-start(f32[2,64,2,64]{3,2,1,0:T(2,128)} %get-tuple-element.5) | copy-start | bytes 196612

commit v4 on v3

--- a/solution.py
+++ b/solution.py
@@ -151,14 +151,13 @@
     return build(len(STEPS), 0, (0, 0))
 
 
-def exact_dot(a, b):
-    return lax.dot_general(
-        a,
-        b,
-        (((1,), (0,)), ((), ())),
-        precision=lax.Precision.HIGHEST,
-        preferred_element_type=jnp.float32,
-    )
+def in_three(x):
+    parts = []
+    for _ in range(3):
+        part = x.astype(jnp.bfloat16)
+        parts.append(part)
+        x = x - part.astype(jnp.float32)
+    return jnp.concatenate(parts, 0)
 
 
 def sample_order():
@@ -202,7 +201,7 @@
 
 
 def pick(places, values):
-    return jnp.where(iota((64, 128), 0) == places, values, 0.0)
+    return jnp.where(iota((192, 128), 0) & 63 == places, values, 0.0)
 
 
 def picks(rank_a, rank_b, count):
@@ -260,6 +259,7 @@
     tiles,
     table,
     halo,
+    chosen,
     listed,
     ids,
     line_sem,
@@ -335,7 +335,6 @@
     take(me, sent[me])
     fetch.wait()
     lane = iota((1, 128), 1)
-    chosen = []
     for r in range(rounds):
         ranks = []
         for c in range(2):
@@ -346,7 +345,9 @@
             for k in range(peers):
                 rank = rank + (own > ids[r * peers + k, me]).astype(jnp.int32)
             ranks.append(rank)
-        chosen.append(ranks)
+        products, powers = picks(*ranks, peers)
+        chosen[r, :128, :] = products.T.astype(jnp.bfloat16)
+        chosen[r, 128:, :] = powers.T.astype(jnp.bfloat16)
     for o in range(1, peers):
         images(o).wait_recv()
         owner = lax.rem(me + peers - o, peers)
@@ -407,15 +408,13 @@
         def _():
             halo[1 - n] = jnp.zeros_like(halo[1 - n])
 
-    matrices = []
     for r in range(rounds):
-        products, powers = picks(*chosen[r], peers)
-        products, powers = products.T, powers.T
-        matrices.append((products, powers))
-        means = exact_dot(products, table[r])
+        means = jnp.dot(
+            chosen[r, :128, :], in_three(table[r]), preferred_element_type=jnp.float32
+        )
         for c in range(2):
             for row in range(2):
-                ifg_ref[r, :, c, row, :] = means[64 * c : 64 * c + 64, 64 * row : 64 * row + 64]
+                ifg_ref[pl.ds(256 * r + 2 * c + row, 64, stride=4), :] = means[64 * c : 64 * c + 64, 64 * row : 64 * row + 64]
 
     for n, (step, there) in enumerate(sides):
 
@@ -424,14 +423,12 @@
             edge(1 - n, step).wait_recv()
 
     for r in range(rounds):
-        products, powers = matrices[r]
         boxed = box_of(table[r], halo[1, r], halo[0, r])
-        parts = exact_dot(products, boxed)
-        power = exact_dot(powers, boxed)
-        size = jnp.sqrt(parts[:64] * parts[:64] + parts[64:] * parts[64:])
-        coherence = size / jnp.sqrt(power[:64] * power[64:])
+        parts = jnp.dot(chosen[r], in_three(boxed), preferred_element_type=jnp.float32)
+        size = jnp.sqrt(parts[:64] * parts[:64] + parts[64:128] * parts[64:128])
+        coherence = size / jnp.sqrt(parts[128:192] * parts[192:])
         for row in range(2):
-            coh_ref[r, :, row, :] = coherence[:, 64 * row : 64 * row + 64]
+            coh_ref[pl.ds(128 * r + row, 64, stride=2), :] = coherence[:, 64 * row : 64 * row + 64]
 
     for o in range(1, peers):
         images(o).wait_send()
@@ -453,11 +450,11 @@
     cells = columns // SAMPLES
     vmem = pl.BlockSpec(memory_space=pltpu.VMEM)
     dma = pltpu.SemaphoreType.DMA
-    return pl.pallas_call(
+    ifg, coh = pl.pallas_call(
         stack_kernel,
         out_shape=(
-            jax.ShapeDtypeStruct((rounds, pair_dev, 2, lines // LINES, cells), jnp.float32),
-            jax.ShapeDtypeStruct((rounds, pair_dev, lines // LINES, cells), jnp.float32),
+            jax.ShapeDtypeStruct((rounds * pair_dev * 2 * lines // LINES, cells), jnp.float32),
+            jax.ShapeDtypeStruct((rounds * pair_dev * lines // LINES, cells), jnp.float32),
         ),
         in_specs=[pl.BlockSpec(memory_space=pl.ANY), vmem],
         out_specs=(vmem, vmem),
@@ -470,6 +467,7 @@
             pltpu.VMEM((peers, rounds, 8, 128), jnp.float32),
             pltpu.VMEM((rounds, 64, 128), jnp.float32),
             pltpu.VMEM((2, rounds, 64, 128), jnp.float32),
+            pltpu.VMEM((rounds, 256, 192), jnp.bfloat16),
             pltpu.VMEM((rounds * peers, 128), jnp.int32),
             pltpu.SMEM((rounds * peers, 128), jnp.int32),
             dma((lines,)),
@@ -483,6 +481,10 @@
         ],
         compiler_params=pltpu.CompilerParams(collective_id=0, has_side_effects=True),
     )(slc, pairs.transpose(0, 2, 1))
+    return (
+        ifg.reshape(rounds, pair_dev, 2, lines // LINES, cells),
+        coh.reshape(rounds, pair_dev, lines // LINES, cells),
+    )
 
 
 def per_device(slc, pairs):

time: 26.2 us -> 26 us (level)
  no operation moved by 1% of the time
where the time goes in v4:
time: 26 us; the launch traced here: 25.8 us
  Pallas kernels  22.8 us (88%)
  local copies, waits for them, and re-layouts  2.36 us (9%)
  between operations  0.65 us (2%)
    pallas_call x1, Pallas kernels, per_device_few(): pl.pallas_call(stack_kernel, out_shape=(jax.ShapeDtypeStruct((rounds * pa...  22.8 us
    unnamed x4, local copies, waits for them, and re-layouts  2.36 us

profile of v4, /device:TPU:1, one launch (start us, length us, event | category | flops | bytes accessed | tf_op | source)
XLA Modules:
  0.0 25.8 jit_solution(4523006801423464885)
XLA Ops:
  0.6 22.8 %shard_map.41 = (f32[512,64]{1,0:T(8,128)}, f32[256,64]{1,0:T(8,128)}) custom-call(f32[6,2,8,1024]{3,2,1,0:T(8,128)} %slc_ref.1, s32[2,2,512]{2,1,0:T(2,128)} %bitcast.5), custom_call_target="tpu_custom_call" | custom-call | tf_op jit(solution)/shard_map/pallas_call | solution.py:453
  23.4 0.0 copy-start
  23.4 1.7 %copy.6 = f32[2,64,2,2,64]{4,3,2,1,0:T(2,128)} copy(f32[2,64,2,2,64]{4,3,2,1,0:T(2,128)} %bitcast.3) | data formatting | bytes 262144
  25.1 0.0 copy-done
  25.1 0.7 %copy.7 = f32[2,64,2,64]{3,2,1,0:T(2,128)} copy(f32[2,64,2,64]{3,2,1,0:T(2,128)S(1)} %bitcast.4) | data formatting | bytes 131072
Async XLA Ops:
  23.4 1.7 %copy-start = (f32[256,64]{1,0:T(8,128)S(1)}, f32[256,64]{1,0:T(8,128)}, u32[]{:S(2)}) copy-start(f32[256,64]{1,0:T(8,128)} %get-tuple-element.5) | copy-start | bytes 196612

commit v5 on v4

--- a/solution.py
+++ b/solution.py
@@ -249,17 +249,16 @@
 def stack_kernel(
     slc_ref,
     pairs_ref,
-    ifg_ref,
-    coh_ref,
+    table,
+    boxed_ref,
+    chosen,
     lines,
     sent,
     held,
     full,
     sums,
     tiles,
-    table,
     halo,
-    chosen,
     listed,
     ids,
     line_sem,
@@ -408,14 +407,6 @@
         def _():
             halo[1 - n] = jnp.zeros_like(halo[1 - n])
 
-    for r in range(rounds):
-        means = jnp.dot(
-            chosen[r, :128, :], in_three(table[r]), preferred_element_type=jnp.float32
-        )
-        for c in range(2):
-            for row in range(2):
-                ifg_ref[pl.ds(256 * r + 2 * c + row, 64, stride=4), :] = means[64 * c : 64 * c + 64, 64 * row : 64 * row + 64]
-
     for n, (step, there) in enumerate(sides):
 
         @pl.when(there)
@@ -423,12 +414,7 @@
             edge(1 - n, step).wait_recv()
 
     for r in range(rounds):
-        boxed = box_of(table[r], halo[1, r], halo[0, r])
-        parts = jnp.dot(chosen[r], in_three(boxed), preferred_element_type=jnp.float32)
-        size = jnp.sqrt(parts[:64] * parts[:64] + parts[64:128] * parts[64:128])
-        coherence = size / jnp.sqrt(parts[128:192] * parts[192:])
-        for row in range(2):
-            coh_ref[pl.ds(128 * r + row, 64, stride=2), :] = coherence[:, 64 * row : 64 * row + 64]
+        boxed_ref[r] = box_of(table[r], halo[1, r], halo[0, r])
 
     for o in range(1, peers):
         images(o).wait_send()
@@ -438,6 +424,25 @@
         @pl.when(there)
         def _():
             edge(n, step).wait_send()
+
+
+def pairs_kernel(table_ref, boxed_ref, chosen_ref, ifg_ref, coh_ref):
+    for r in range(table_ref.shape[0]):
+        means = jnp.dot(
+            chosen_ref[r, :128, :], in_three(table_ref[r]), preferred_element_type=jnp.float32
+        )
+        for c in range(2):
+            for row in range(2):
+                part = means[64 * c : 64 * c + 64, 64 * row : 64 * row + 64]
+                ifg_ref[pl.ds(256 * r + 2 * c + row, 64, stride=4), :] = part
+        parts = jnp.dot(
+            chosen_ref[r], in_three(boxed_ref[r]), preferred_element_type=jnp.float32
+        )
+        size = jnp.sqrt(parts[:64] * parts[:64] + parts[64:128] * parts[64:128])
+        coherence = size / jnp.sqrt(parts[128:192] * parts[192:])
+        for row in range(2):
+            part = coherence[:, 64 * row : 64 * row + 64]
+            coh_ref[pl.ds(128 * r + row, 64, stride=2), :] = part
 
 
 def per_device_few(slc, pairs):
@@ -450,14 +455,15 @@
     cells = columns // SAMPLES
     vmem = pl.BlockSpec(memory_space=pltpu.VMEM)
     dma = pltpu.SemaphoreType.DMA
-    ifg, coh = pl.pallas_call(
+    found = pl.pallas_call(
         stack_kernel,
         out_shape=(
-            jax.ShapeDtypeStruct((rounds * pair_dev * 2 * lines // LINES, cells), jnp.float32),
-            jax.ShapeDtypeStruct((rounds * pair_dev * lines // LINES, cells), jnp.float32),
+            jax.ShapeDtypeStruct((rounds, 64, 128), jnp.float32),
+            jax.ShapeDtypeStruct((rounds, 64, 128), jnp.float32),
+            jax.ShapeDtypeStruct((rounds, 256, 192), jnp.bfloat16),
         ),
         in_specs=[pl.BlockSpec(memory_space=pl.ANY), vmem],
-        out_specs=(vmem, vmem),
+        out_specs=(vmem,) * 3,
         scratch_shapes=[
             pltpu.VMEM(slc.shape, jnp.float32),
             pltpu.VMEM((peers, rows, width), jnp.bfloat16),
@@ -465,9 +471,7 @@
             pltpu.VMEM((peers * date_dev * 2, lines, width), jnp.float32),
             pltpu.VMEM((peers, rounds, 8, 128), jnp.float32),
             pltpu.VMEM((peers, rounds, 8, 128), jnp.float32),
-            pltpu.VMEM((rounds, 64, 128), jnp.float32),
             pltpu.VMEM((2, rounds, 64, 128), jnp.float32),
-            pltpu.VMEM((rounds, 256, 192), jnp.bfloat16),
             pltpu.VMEM((rounds * peers, 128), jnp.int32),
             pltpu.SMEM((rounds * peers, 128), jnp.int32),
             dma((lines,)),
@@ -481,6 +485,15 @@
         ],
         compiler_params=pltpu.CompilerParams(collective_id=0, has_side_effects=True),
     )(slc, pairs.transpose(0, 2, 1))
+    ifg, coh = pl.pallas_call(
+        pairs_kernel,
+        out_shape=(
+            jax.ShapeDtypeStruct((rounds * pair_dev * 2 * lines // LINES, cells), jnp.float32),
+            jax.ShapeDtypeStruct((rounds * pair_dev * lines // LINES, cells), jnp.float32),
+        ),
+        in_specs=[vmem] * 3,
+        out_specs=(vmem, vmem),
+    )(*found)
     return (
         ifg.reshape(rounds, pair_dev, 2, lines // LINES, cells),
         coh.reshape(rounds, pair_dev, lines // LINES, cells),

time: 26 us -> 25.4 us (0.977)
  local copies, waits for them, and re-layouts: 2.36 us -> 0 us
  Pallas kernels: 22.8 us -> 24.5 us
    unnamed x4 -> x0, local copies, waits for them, and re-layouts: 2.36 us -> none
    pallas_call x1 -> x2, Pallas kernels: 22.8 us -> 24.5 us  [the longest x1 22.5 us: per_device_few(): pl.pallas_call(stack_kernel, out_shape=(jax.ShapeDtypeStruct((rounds, 64,...]
where the time goes in v5:
time: 25.4 us; the launch traced here: 25.1 us
  Pallas kernels  24.5 us (96%)
  between operations  0.64 us (3%)
    pallas_call x1, Pallas kernels, per_device_few(): pl.pallas_call(stack_kernel, out_shape=(jax.ShapeDtypeStruct((rounds, 64,...  22.5 us
    pallas_call x1, Pallas kernels, per_device_few(): pl.pallas_call(pairs_kernel, out_shape=(jax.ShapeDtypeStruct((rounds * pa...  2.03 us

profile of v5, /device:TPU:1, one launch (start us, length us, event | category | flops | bytes accessed | tf_op | source)
XLA Modules:
  0.0 25.1 jit_solution(6914397145272116604)
XLA Ops:
  0.6 22.5 %shard_map.41 = (f32[2,64,128]{2,1,0:T(8,128)}, f32[2,64,128]{2,1,0:T(8,128)}, bf16[2,256,192]{2,1,0:T(8,128)(2,1)}) custom-call(f32[6,2,8,1024]{3,2,1,0:T(8,128)} %slc_ref.1, s32[2,2,512]{2,1,0:T(2,128)} %bitcast.3), custom_call_target="tpu_custom_call" | custom-call | tf_op jit(solution)/shard_map/pallas_call | solution.py:458
  23.1 2.0 %shard_map.42 = (f32[512,64]{1,0:T(8,128)}, f32[256,64]{1,0:T(8,128)}) custom-call(f32[2,64,128]{2,1,0:T(8,128)} %get-tuple-element.7.table_ref, f32[2,64,128]{2,1,0:T(8,128)} %get-tuple-element.8.boxed_ref, bf16[2,256,192]{2,1,0:T(8,128)(2,1)} %get-tuple-element.9.chosen_ref), custom_call_target="tpu_custom_call" | custom-call | tf_op jit(solution)/shard_map/pallas_call | solution.py:488

commit v6 on v5

--- a/solution.py
+++ b/solution.py
@@ -1,3 +1,4 @@
+import functools
 import jax
 import jax.numpy as jnp
 from jax import lax
@@ -352,20 +353,20 @@
         owner = lax.rem(me + peers - o, peers)
         take(owner, held[owner])
 
-    def results(o):
+    def results(o, r):
         peer = lax.rem(me + o, peers)
         return pltpu.make_async_remote_copy(
-            src_ref=sums.at[peer],
-            dst_ref=tiles.at[me],
-            send_sem=send_b.at[o],
-            recv_sem=recv_b.at[o],
+            src_ref=sums.at[peer, r],
+            dst_ref=tiles.at[me, r],
+            send_sem=send_b.at[r, o],
+            recv_sem=recv_b.at[r, o],
             device_id={"date": peer},
             device_id_type=MESH,
         )
 
-    def serve(o, carry):
-        peer = lax.rem(me + o, peers)
-        for r in range(rounds):
+    def serve(r, half, carry):
+        for o in (2 * half + 1, 2 * half + 2):
+            peer = lax.rem(me + o, peers)
             real, imag = [], []
             for k in range(peers):
                 date = ids[r * peers + k, peer]
@@ -373,57 +374,64 @@
                 imag.append(full[2 * date + 1])
             sums[peer, r] = cell_sums(real, imag)
 
-        @pl.when(o < peers)
+        results(2 * half + 1, r).start()
+
+        @pl.when(half < peers // 2 - 1)
         def _():
-            results(o).start()
+            results(2 * half + 2, r).start()
 
         return carry
 
-    lax.fori_loop(1, peers + 1, serve, 0)
+    for r in range(rounds):
+        lax.fori_loop(0, peers // 2, functools.partial(serve, r), 0)
     tiles[me] = sums[me]
-    for o in range(1, peers):
-        results(o).wait_recv()
-    for r in range(rounds):
-        for k, tile in enumerate(table_of([tiles[j, r] for j in range(peers)])):
-            table[r, 8 * k : 8 * k + 8, :] = tile
-
-    def edge(n, step):
+
+    def edge(n, step, r):
         return pltpu.make_async_remote_copy(
-            src_ref=table,
-            dst_ref=halo.at[n],
-            send_sem=send_h.at[n],
-            recv_sem=recv_h.at[n],
+            src_ref=table.at[r],
+            dst_ref=halo.at[n, r],
+            send_sem=send_h.at[n, r],
+            recv_sem=recv_h.at[n, r],
             device_id={"az": az + step},
             device_id_type=MESH,
         )
 
     for n, (step, there) in enumerate(sides):
-
-        @pl.when(there)
-        def _():
-            edge(n, step).start()
 
         @pl.when(jnp.logical_not(there))
         def _():
             halo[1 - n] = jnp.zeros_like(halo[1 - n])
 
+    for r in range(rounds):
+        for o in range(1, peers):
+            results(o, r).wait_recv()
+        for k, tile in enumerate(table_of([tiles[j, r] for j in range(peers)])):
+            table[r, 8 * k : 8 * k + 8, :] = tile
+        for n, (step, there) in enumerate(sides):
+
+            @pl.when(there)
+            def _():
+                edge(n, step, r).start()
+
+    for r in range(rounds):
+        for n, (step, there) in enumerate(sides):
+
+            @pl.when(there)
+            def _():
+                edge(1 - n, step, r).wait_recv()
+
+        boxed_ref[r] = box_of(table[r], halo[1, r], halo[0, r])
+
+    for o in range(1, peers):
+        images(o).wait_send()
+        for r in range(rounds):
+            results(o, r).wait_send()
     for n, (step, there) in enumerate(sides):
 
         @pl.when(there)
         def _():
-            edge(1 - n, step).wait_recv()
-
-    for r in range(rounds):
-        boxed_ref[r] = box_of(table[r], halo[1, r], halo[0, r])
-
-    for o in range(1, peers):
-        images(o).wait_send()
-        results(o).wait_send()
-    for n, (step, there) in enumerate(sides):
-
-        @pl.when(there)
-        def _():
-            edge(n, step).wait_send()
+            for r in range(rounds):
+                edge(n, step, r).wait_send()
 
 
 def pairs_kernel(table_ref, boxed_ref, chosen_ref, ifg_ref, coh_ref):
@@ -477,10 +485,10 @@
             dma((lines,)),
             dma((peers,)),
             dma((peers,)),
-            dma((peers,)),
-            dma((peers,)),
-            dma((2,)),
-            dma((2,)),
+            dma((rounds, peers)),
+            dma((rounds, peers)),
+            dma((2, rounds)),
+            dma((2, rounds)),
             dma,
         ],
         compiler_params=pltpu.CompilerParams(collective_id=0, has_side_effects=True),

time: 25.4 us -> 26.7 us (1.051)
  Pallas kernels: 24.5 us -> 25.8 us
    pallas_call x1, Pallas kernels: 22.5 us -> 23.8 us  [per_device_few(): pl.pallas_call(stack_kernel, out_shape=(jax.ShapeDtypeStruct((rounds, 64,...]
where the time goes in v6:
time: 26.7 us; the launch traced here: 26.5 us
  Pallas kernels  25.8 us (97%)
  between operations  0.64 us (2%)
    pallas_call x1, Pallas kernels, per_device_few(): pl.pallas_call(stack_kernel, out_shape=(jax.ShapeDtypeStruct((rounds, 64,...  23.8 us
    pallas_call x1, Pallas kernels, per_device_few(): pl.pallas_call(pairs_kernel, out_shape=(jax.ShapeDtypeStruct((rounds * pa...  2.03 us

profile of v6, /device:TPU:1, one launch (start us, length us, event | category | flops | bytes accessed | tf_op | source)
XLA Modules:
  0.0 26.5 jit_solution(12253564365242977005)
XLA Ops:
  0.6 23.8 %shard_map.41 = (f32[2,64,128]{2,1,0:T(8,128)}, f32[2,64,128]{2,1,0:T(8,128)}, bf16[2,256,192]{2,1,0:T(8,128)(2,1)}) custom-call(f32[6,2,8,1024]{3,2,1,0:T(8,128)} %slc_ref.1, s32[2,2,512]{2,1,0:T(2,128)} %bitcast.3), custom_call_target="tpu_custom_call" | custom-call | tf_op jit(solution)/shard_map/pallas_call | solution.py:466
  24.4 2.0 %shard_map.42 = (f32[512,64]{1,0:T(8,128)}, f32[256,64]{1,0:T(8,128)}) custom-call(f32[2,64,128]{2,1,0:T(8,128)} %get-tuple-element.7.table_ref, f32[2,64,128]{2,1,0:T(8,128)} %get-tuple-element.8.boxed_ref, bf16[2,256,192]{2,1,0:T(8,128)(2,1)} %get-tuple-element.9.chosen_ref), custom_call_target="tpu_custom_call" | custom-call | tf_op jit(solution)/shard_map/pallas_call | solution.py:496

commit v7 on v5

--- a/solution.py
+++ b/solution.py
@@ -290,18 +290,17 @@
             pl.semaphore_signal(barrier, inc=1, device_id={"az": az + step}, device_id_type=MESH)
 
     def line(n):
-        row = n % LINES * 2 + n // LINES
-        return pltpu.make_async_copy(
-            slc_ref.at[:, :, n, :], lines.at[:, :, row, :], line_sem.at[n]
-        )
-
-    for n in range(2 * LINES):
+        return pltpu.make_async_copy(slc_ref.at[n], lines.at[n], line_sem.at[n])
+
+    for n in range(date_dev):
         line(n).start()
-    for n in range(2 * LINES):
+    rows_date = sent.shape[1] // date_dev
+    for n in range(date_dev):
         line(n).wait()
-    for j in range(peers):
-        part = lines[:, :, :, j * width : (j + 1) * width]
-        sent[j] = part.reshape(sent.shape[1:]).astype(jnp.bfloat16)
+        for j in range(peers):
+            part = lines[n, :, :, j * width : (j + 1) * width]
+            at = slice(n * rows_date, (n + 1) * rows_date)
+            sent[j, at] = part.reshape(rows_date, width).astype(jnp.bfloat16)
     greeted = peers - 1 + (az > 0).astype(jnp.int32) + (az < az_size - 1).astype(jnp.int32)
     pl.semaphore_wait(barrier, greeted)
 
@@ -328,8 +327,11 @@
 
     def take(owner, block):
         spread = jnp.dot(block, order, preferred_element_type=jnp.float32)
-        at = pl.ds(owner * images_dev, images_dev)
-        full[at] = spread.reshape((images_dev,) + full.shape[1:])
+        for image in range(images_dev):
+            for group in range(2):
+                row = image * 8 + group * LINES
+                at = (owner * images_dev + image, pl.ds(group, LINES, stride=2))
+                full[at] = spread[row : row + LINES]
 
     take(me, sent[me])
     fetch.wait()
@@ -474,7 +476,7 @@
             pltpu.VMEM((2, rounds, 64, 128), jnp.float32),
             pltpu.VMEM((rounds * peers, 128), jnp.int32),
             pltpu.SMEM((rounds * peers, 128), jnp.int32),
-            dma((lines,)),
+            dma((date_dev,)),
             dma((peers,)),
             dma((peers,)),
             dma((peers,)),

time: 25.4 us -> 25.4 us (level)
  no operation moved by 1% of the time
where the time goes in v7:
time: 25.4 us; the launch traced here: 25.1 us
  Pallas kernels  24.5 us (96%)
  between operations  0.64 us (3%)
    pallas_call x1, Pallas kernels, per_device_few(): pl.pallas_call(stack_kernel, out_shape=(jax.ShapeDtypeStruct((rounds, 64,...  22.5 us
    pallas_call x1, Pallas kernels, per_device_few(): pl.pallas_call(pairs_kernel, out_shape=(jax.ShapeDtypeStruct((rounds * pa...  2.03 us

profile of v7, /device:TPU:1, one launch (start us, length us, event | category | flops | bytes accessed | tf_op | source)
XLA Modules:
  0.0 25.1 jit_solution(11694071841325722042)
XLA Ops:
  0.6 22.5 %shard_map.41 = (f32[2,64,128]{2,1,0:T(8,128)}, f32[2,64,128]{2,1,0:T(8,128)}, bf16[2,256,192]{2,1,0:T(8,128)(2,1)}) custom-call(f32[6,2,8,1024]{3,2,1,0:T(8,128)} %slc_ref.1, s32[2,2,512]{2,1,0:T(2,128)} %bitcast.3), custom_call_target="tpu_custom_call" | custom-call | tf_op jit(solution)/shard_map/pallas_call | solution.py:460
  23.1 2.0 %shard_map.42 = (f32[512,64]{1,0:T(8,128)}, f32[256,64]{1,0:T(8,128)}) custom-call(f32[2,64,128]{2,1,0:T(8,128)} %get-tuple-element.7.table_ref, f32[2,64,128]{2,1,0:T(8,128)} %get-tuple-element.8.boxed_ref, bf16[2,256,192]{2,1,0:T(8,128)(2,1)} %get-tuple-element.9.chosen_ref), custom_call_target="tpu_custom_call" | custom-call | tf_op jit(solution)/shard_map/pallas_call | solution.py:490
